TPU v7x, 32 devices: a whole 2x2x4 slice. The times are simulated.
32 devices in a mesh: grp: 2 (over x), dp: 4 (over y, core), mp: 4 (over z).
Axes of the slice: x: 2, y: 2, z: 4, core: 2. Of those that a mesh axis runs over, the one named last changes fastest.
Arguments:
- up_input: bfloat16 [8, 256, 4096], P(('grp', 'dp'), None, 'mp'), may hold values from -6 to 6
- gate_pre: bfloat16 [8, 256, 14336], P(('grp', 'dp'), None, 'mp'), may hold values from -6 to 6
- up_pre: bfloat16 [8, 256, 14336], P(('grp', 'dp'), None, 'mp'), may hold values from -6 to 6
- grad_hidden: bfloat16 [8, 256, 14336], P(('grp', 'dp'), None, 'mp'), may hold values from -6 to 6
- grad_output: bfloat16 [8, 256, 4096], P(('grp', 'dp'), None, 'mp'), may hold values from -6 to 6
- proj_up_in: bfloat16 [64, 4096], P(None, 'mp'), may hold values from -0.09375 to 0.09375
- proj_up_out: bfloat16 [64, 14336], P(None, 'mp'), may hold values from -0.046875 to 0.046875
- proj_down_in: bfloat16 [64, 14336], P(None, 'mp'), may hold values from -0.046875 to 0.046875
- proj_down_out: bfloat16 [64, 4096], P(None, 'mp'), may hold values from -0.09375 to 0.09375
- gram: float32 [8192, 8192], P(('grp', 'mp'), 'dp'), may hold values from -4 to 14
- canaries: bfloat16 [1024, 8192], P('dp', ('grp', 'mp')), may hold values from -6 to 6
Outputs:
- gram_new: float32 [8192, 8192], P(('grp', 'mp'), 'dp')
- mapped: bfloat16 [1024, 8192], P(('grp', 'mp'), 'dp')
- scores: float32 [8, 1024], P(None, ('grp', 'mp'))
All inputs are finite; a program needn't handle non-finite values.
Results may differ from a plain program's by a relative error of at most 0.005.
Values may be sent and summed in bfloat16 or wider, within the bound.
No kernel may reach another device: no remote copies, remote signals or barrier semaphores. Data moves between devices by JAX's collectives and lax.ppermute only.
A program may use at most 64 MiB of HBM per device.

v0:
```python
import math

import jax
import jax.numpy as jnp
from jax import lax
from jax.sharding import PartitionSpec as P


def project(values, matrix):
    return lax.dot_general(
        values, matrix, (((1,), (1,)), ((), ())), preferred_element_type=jnp.float32
    )


def shards(
    up_input,
    gate_pre,
    up_pre,
    grad_hidden,
    grad_output,
    proj_up_in,
    proj_up_out,
    proj_down_in,
    proj_down_out,
    gram,
    canaries,
):
    seq_len = up_input.shape[1]
    gate_act = jax.nn.silu(gate_pre[0].astype(jnp.float32))
    grad_up = (grad_hidden[0].astype(jnp.float32) * gate_act).astype(jnp.bfloat16)
    hidden = (gate_act * up_pre[0].astype(jnp.float32)).astype(jnp.bfloat16)
    in_up, out_up, in_down, out_down = lax.psum(
        (
            project(up_input[0], proj_up_in),
            project(grad_up, proj_up_out),
            project(hidden, proj_down_in),
            project(grad_output[0], proj_down_out),
        ),
        "mp",
    )
    norm_len = 1.0 / math.sqrt(seq_len)
    up_feat = jnp.dot(out_up.T, in_up, precision=lax.Precision.HIGHEST) * norm_len
    down_feat = jnp.dot(out_down.T, in_down, precision=lax.Precision.HIGHEST) * norm_len
    own_row = jnp.concatenate([up_feat.reshape(-1), down_feat.reshape(-1)])[None, :]
    feature_rows = lax.all_gather(own_row, ("grp", "dp"), axis=0, tiled=True)
    seq_total = feature_rows.shape[0]
    feature_count = feature_rows.shape[1]
    rows_here = gram.shape[0]
    cols_here = gram.shape[1]
    block_row = lax.axis_index("grp") * lax.axis_size("mp") + lax.axis_index("mp")
    block_col = lax.axis_index("dp")
    left_block = lax.dynamic_slice_in_dim(feature_rows, block_row * rows_here, rows_here, 1)
    right_block = lax.dynamic_slice_in_dim(feature_rows, block_col * cols_here, cols_here, 1)
    gram_new = (
        gram + jnp.dot(left_block.T, right_block, precision=lax.Precision.HIGHEST) / seq_total
    )
    gram_low = gram_new.astype(jnp.bfloat16)
    norm_order = 1.0 / math.sqrt(feature_count)
    gathered = lax.all_gather(canaries, "dp", axis=0, tiled=True)
    mapped_share = (
        lax.psum_scatter(
            jnp.dot(gathered, gram_low, preferred_element_type=jnp.float32),
            ("grp", "mp"),
            scatter_dimension=0,
            tiled=True,
        )
        * norm_order
    )
    scores = lax.psum(
        jnp.dot(right_block, mapped_share.T, precision=lax.Precision.HIGHEST) * norm_order, "dp"
    )
    return (gram_new, mapped_share.astype(jnp.bfloat16), scores)


def solution(mesh):
    return jax.shard_map(
        shards,
        mesh=mesh,
        in_specs=(
            P(("grp", "dp"), None, "mp"),
            P(("grp", "dp"), None, "mp"),
            P(("grp", "dp"), None, "mp"),
            P(("grp", "dp"), None, "mp"),
            P(("grp", "dp"), None, "mp"),
            P(None, "mp"),
            P(None, "mp"),
            P(None, "mp"),
            P(None, "mp"),
            P(("grp", "mp"), "dp"),
            P("dp", ("grp", "mp")),
        ),
        out_specs=(P(("grp", "mp"), "dp"), P(("grp", "mp"), "dp"), P(None, ("grp", "mp"))),
        check_vma=False,
    )
```

profile of v0, /device:TPU:0, one launch (start us, length us, event | category | flops | bytes accessed | tf_op | source)
XLA Modules:
  0.0 262.6 jit_solution(10737673905319260418)
XLA Ops:
  8.0 0.0 copy-start
  8.0 0.0 all-reduce.3.cloned.1.call-start
  8.1 1.0 copy-done
  9.0 1.9 fusion.15
  10.9 4.1 %fusion.8 = f32[256,64]{1,0:T(8,128)} fusion(bf16[64,3584]{1,0:T(8,128)(2,1)} %param.18, bf16[1,256,3584]{2,1,0:T(8,128)(2,1)} %param.13, bf16[1,256,3584]{2,1,0:T(8,128)(2,1)} %param.12), kind=kOutput, calls=%fused_computation.13 | convolution fusion | flops 124780544 | bytes 4194304 | tf_op jit(solution)/shard_map/dot_general | solution.py:10
  15.0 0.0 copy-done.3
  15.0 0.0 copy-done.4
  15.0 0.0 copy-done.5
  15.0 0.0 copy-start.1
  15.0 0.0 copy-start.2
  15.0 1.8 fusion.6
  16.9 0.0 copy-done.1
  16.9 0.9 fusion.13
  17.8 0.0 all-reduce.3.cloned.1.call-update
  17.9 0.0 all-gather.3.cloned.1.call-start
  17.9 0.5 all-gather.3.cloned.1.call-update
  18.4 0.0 reduce-scatter.2.cloned.1.call-start
  18.5 41.2 %all-reduce.3.cloned.1.call-done = (f32[256,64]{1,0:T(8,128)}, f32[256,64]{1,0:T(8,128)}, f32[256,64]{1,0:T(8,128)}, f32[256,64]{1,0:T(8,128)}) async-done(((f32[256,64]{1,0:T(8,128)}, f32[256,64]{1,0:T(8,128)}, f32[256,64]{1,0:T(8,128)}, f32[256,64]{1,0:T(8,128)}), (f32[256,64]{1,0:T(8,128)}, f32[256,64]{1,0:T(8,128)}, f32[256,64]{1,0:T(8,128)}, f32[256,64]{1,0:T(8,128)})) %all-reduce.3.cloned.1.call-update) | async-done | bytes 262160 | tf_op jit(solution)/shard_map/psum | solution.py:32
  59.7 1.3 convolution_multiply_fusion
  61.1 0.1 reshape.19
  61.1 1.3 convolution_multiply_fusion.1
  62.5 0.1 reshape.18
  62.6 9.3 %all-gather = f32[65536]{0:T(1024)S(1)} all-gather(f32[8192]{0:T(1024)S(1)} %pad_maximum_fusion), channel_id=2, replica_groups=mesh['grp'=2,'dp'=4,'mp'=4] {'grp','dp'}, dimensions={0}, use_global_device_ids=true | all-gather | bytes 294912 | tf_op jit(solution)/shard_map/all_gather | solution.py:45
  71.9 0.1 reshape.23
  71.9 11.4 %multiply_add_fusion = f32[1024,2048]{1,0:T(8,128)} fusion(f32[1024,2048]{1,0:T(8,128)} %param.20, f32[8,8192]{1,0:T(8,128)S(1)} %reshape.23, s32[]{:T(128)S(6)} %select_n.7, s32[]{:T(128)S(6)} %select_n.6), kind=kOutput, calls=%fused_computation | convolution fusion | flops 205520896 | bytes 16875528 | tf_op jit(solution)/shard_map/dot_general | solution.py:55
  83.3 11.8 %convolution_bitcast_fusion = f32[1024,2048]{0,1:T(8,128)} fusion(bf16[1024,1024]{1,0:T(8,128)(2,1)} %all-gather.3.cloned.1.call-done, f32[1024,2048]{1,0:T(8,128)} %multiply_add_fusion), kind=kOutput, calls=%fused_computation.3 | convolution fusion | flops 4297064448 | bytes 18874368 | tf_op jit(solution)/shard_map/dot_general | solution.py:62
  95.1 0.0 reduce-scatter.2.cloned.1.call-update
  95.1 148.4 %reduce-scatter.2.cloned.1.call-done = f32[128,2048]{0,1:T(8,128)} async-done(((f32[1024,2048]{0,1:T(8,128)}), f32[128,2048]{0,1:T(8,128)}) %reduce-scatter.2.cloned.1.call-update) | async-done | bytes 1048592 | tf_op jit(solution)/shard_map/reduce_scatter | solution.py:61
  243.6 1.3 multiply_convert_fusion
  244.9 1.0 copy.15
  245.9 1.9 convolution_multiply_fusion.2
  247.8 7.4 %psum.39 = f32[8,128]{1,0:T(8,128)} all-reduce(f32[8,128]{1,0:T(8,128)S(1)} %convolution_multiply_fusion.2), channel_id=1, replica_groups=mesh['grp'=2,'dp'=4,'mp'=4] {'dp'}, use_global_device_ids=true, to_apply=%region_5.6 | all-reduce | flops 1024 | bytes 8192 | tf_op jit(solution)/shard_map/psum | solution.py:69
  (6 shorter events, 0.0 us)
Async XLA Ops:
  8.0 1.0 copy-start
  8.0 51.7 %all-reduce.3.cloned.1.call-start = ((), (), s32[]{:S(2)}) async-start(), calls=%async_computation.3 | async-start | bytes 1048576 | tf_op jit(solution)/shard_map/psum | solution.py:32
  10.9 4.1 %copy-start.3 = (bf16[1,256,3584]{2,1,0:T(8,128)(2,1)S(1)}, bf16[1,256,3584]{2,1,0:T(8,128)(2,1)}, u32[]{:S(2)}) copy-start(bf16[1,256,3584]{2,1,0:T(8,128)(2,1)} %param.12) | copy-start | bytes 5505028
  10.9 4.1 %copy-start.4 = (bf16[1,256,3584]{2,1,0:T(8,128)(2,1)S(1)}, bf16[1,256,3584]{2,1,0:T(8,128)(2,1)}, u32[]{:S(2)}) copy-start(bf16[1,256,3584]{2,1,0:T(8,128)(2,1)} %param.14) | copy-start | bytes 5505028
  10.9 4.1 %copy-start.5 = (bf16[64,3584]{1,0:T(8,128)(2,1)S(1)}, bf16[64,3584]{1,0:T(8,128)(2,1)}, u32[]{:S(2)}) copy-start(bf16[64,3584]{1,0:T(8,128)(2,1)} %param.17) | copy-start | bytes 1376260
  15.0 1.9 copy-start.1
  15.0 1.9 copy-start.2
  17.9 65.5 %all-gather.3.cloned.1.call-start = ((), (), s32[]{:S(2)}) async-start(), calls=%async_computation.1 | async-start | bytes 2621440 | tf_op jit(solution)/shard_map/all_gather | solution.py:59
  18.4 225.1 %reduce-scatter.2.cloned.1.call-start = ((), (), s32[]{:S(2)}) async-start(), calls=%async_computation.2 | async-start | bytes 9437184 | tf_op jit(solution)/shard_map/reduce_scatter | solution.py:61
Sparse Core Ops, SparseCore 0:
  18.0 41.6 all-reduce.2
  95.3 148.2 reduce-scatter.1
Sparse Core Ops, SparseCore 1:
  19.9 25.1 all-gather.2
where the time goes:
time: 263 us
  waiting for transfers between devices  190 us (72%)
  matrix products  36.5 us (14%)
  blocking collectives  16.8 us (6%)
  between operations  15.6 us (6%)
    reduce_scatter x1, waiting for transfers between devices, shards(): lax.psum_scatter(jnp.dot(gathered, gram_low, preferred_element_type=jnp.f...  148 us
    psum x1, waiting for transfers between devices, shards(): lax.psum((project(up_input[0], proj_up_in), project(grad_up, proj_up_out)...  41.2 us
    dot_general x1, matrix products, shards(): jnp.dot(gathered, gram_low, preferred_element_type=jnp.float32)  11.8 us
    dot_general x1, matrix products, shards(): jnp.dot(left_block.T, right_block, precision=lax.Precision.HIGHEST)  11.4 us
    all_gather x1, blocking collectives, shards(): feature_rows = lax.all_gather(own_row, ('grp', 'dp'), axis=0, tiled=True)  9.33 us
    dot_general x4, matrix products, project(): lax.dot_general(values, matrix, (((1,), (1,)), ((), ())), preferred_eleme...  8.74 us
    psum x1, blocking collectives, shards(): lax.psum(jnp.dot(right_block, mapped_share.T, precision=lax.Precision.HIG...  7.42 us
  transfers between devices with their start and end apart: 3, of which 2 were waited for; matrix products, arithmetic and copies ran while one was open for 5% of the time, Pallas kernels for 0%

commit v1 on v0

v1 whole, which is shorter than its diff:
```python
import functools
import math

import jax
import jax.numpy as jnp
from jax import lax
from jax.experimental import pallas as pl
from jax.experimental.pallas import tpu as pltpu
from jax.sharding import PartitionSpec as P

LANES = 128
NT = (((1,), (1,)), ((), ()))
TN = (((0,), (0,)), ((), ()))
VMEM_LIMIT = 48 * 1024 * 1024


def dot(a, b, dims, precision=None):
    return lax.dot_general(a, b, dims, precision=precision, preferred_element_type=jnp.float32)


def pairs(size, bit):
    return [(at, at ^ bit) for at in range(size)]


def bits_of(size):
    return [1 << at for at in reversed(range(size.bit_length() - 1))]


def params():
    return pltpu.CompilerParams(vmem_limit_bytes=VMEM_LIMIT)


def cost(flops, bytes_accessed):
    return pl.CostEstimate(flops=flops, bytes_accessed=bytes_accessed, transcendentals=0)


def project_kernel(mp, me, up_in, gate, up_pre, grad_h, grad_o, p_ui, p_uo, p_di, p_do, *rest):
    outs, (whole, out_up, in_down) = rest[:mp], rest[mp:]
    step = pl.program_id(0)
    act = gate[...].astype(jnp.float32)
    act = act / (1.0 + jnp.exp(-act))
    grad_up = (grad_h[...].astype(jnp.float32) * act).astype(jnp.bfloat16)
    hidden = (act * up_pre[...].astype(jnp.float32)).astype(jnp.bfloat16)
    part_up = dot(grad_up, p_uo[...], NT)
    part_down = dot(hidden, p_di[...], NT)

    @pl.when(step == 0)
    def _():
        out_up[...] = part_up
        in_down[...] = part_down

    @pl.when(step > 0)
    def _():
        out_up[...] += part_up
        in_down[...] += part_down

    @pl.when(step == pl.num_programs(0) - 1)
    def _():
        in_up = dot(up_in[...], p_ui[...], NT)
        out_down = dot(grad_o[...], p_do[...], NT)
        whole[...] = jnp.concatenate([in_up, out_up[...], in_down[...], out_down], axis=1)
        rows = outs[0].shape[0]
        own = me[0] % mp
        for at, out in enumerate(outs):
            out[...] = whole[pl.ds(pl.multiple_of((own ^ at) * rows, rows), rows), :]


def project_all(mp, me, up_in, gate, up_pre, grad_h, grad_o, p_ui, p_uo, p_di, p_do):
    _, seq, d_here = up_in.shape
    f_here = gate.shape[2]
    rank = p_ui.shape[0]
    tile = max(t for t in range(LANES, 897, LANES) if f_here % t == 0)
    wide = pl.BlockSpec((None, seq, tile), lambda i, me: (0, 0, i))
    narrow = pl.BlockSpec((None, seq, d_here), lambda i, me: (0, 0, 0))
    wide_p = pl.BlockSpec((rank, tile), lambda i, me: (0, i))
    narrow_p = pl.BlockSpec((rank, d_here), lambda i, me: (0, 0))
    rows = seq // mp
    return pl.pallas_call(
        functools.partial(project_kernel, mp),
        out_shape=[jax.ShapeDtypeStruct((rows, 4 * rank), jnp.float32)] * mp,
        grid_spec=pltpu.PrefetchScalarGridSpec(
            num_scalar_prefetch=1,
            grid=(f_here // tile,),
            in_specs=[narrow, wide, wide, wide, narrow, narrow_p, wide_p, wide_p, narrow_p],
            out_specs=[pl.BlockSpec((rows, 4 * rank), lambda i, me: (0, 0))] * mp,
            scratch_shapes=[
                pltpu.VMEM((seq, 4 * rank), jnp.float32),
                pltpu.VMEM((seq, rank), jnp.float32),
                pltpu.VMEM((seq, rank), jnp.float32),
            ],
        ),
        compiler_params=params(),
        cost_estimate=cost(4 * seq * rank * (d_here + f_here), 6 * seq * f_here + 4 * seq * d_here),
    )(me, up_in, gate, up_pre, grad_h, grad_o, p_ui, p_uo, p_di, p_do)


def feature_kernel(norm, rank, *refs):
    parts, out, (square,) = refs[:-2], refs[-2], refs[-1:]
    total = parts[0][...]
    for part in parts[1:]:
        total = total + part[...]
    half = rank * rank // LANES
    for at in range(2):
        left = total[:, (2 * at + 1) * rank : (2 * at + 2) * rank]
        right = total[:, 2 * at * rank : (2 * at + 1) * rank]
        square[...] = dot(left, right, TN, lax.Precision.HIGHEST) * norm
        step = LANES // rank
        out[at * half : (at + 1) * half, :] = jnp.concatenate(
            [square[pl.ds(lane, half, step), :] for lane in range(step)], axis=1
        )


def feature_rows(norm, rank, parts):
    return pl.pallas_call(
        functools.partial(feature_kernel, norm, rank),
        out_shape=jax.ShapeDtypeStruct((2 * rank * rank // LANES, LANES), jnp.float32),
        scratch_shapes=[pltpu.VMEM((rank, rank), jnp.float32)],
        compiler_params=params(),
        cost_estimate=cost(24 * rank * rank * parts[0].shape[0], 100000),
    )(*parts)


def spread_kernel(seqs, dp, mp, me, gathered, left, right, thin, col, rows_f, cols_f):
    grp_at, dp_at, mp_at = me[0] // (dp * mp), (me[0] // mp) % dp, me[0] % mp
    own = grp_at * dp + dp_at
    row_at = grp_at * mp + mp_at
    count = seqs.bit_length() - 1
    row_groups, col_groups = rows_f.shape[1] // LANES, cols_f.shape[1] // LANES
    for seq in range(seqs):
        code = own ^ seq
        place = 0
        for bit in range(count):
            place = place + (((code >> bit) & 1) << (count - 1 - bit))
        for group in range(row_groups):
            rows_f[seq : seq + 1, group * LANES : (group + 1) * LANES] = gathered[
                place, pl.ds(row_at * row_groups + group, 1), :
            ]
        for group in range(col_groups):
            cols_f[seq : seq + 1, group * LANES : (group + 1) * LANES] = gathered[
                place, pl.ds(dp_at * col_groups + group, 1), :
            ]
    row, column = rows_f[...], cols_f[...]
    row_high = row.astype(jnp.bfloat16).astype(jnp.float32)
    col_high = column.astype(jnp.bfloat16).astype(jnp.float32)
    row_low, col_low = row - row_high, column - col_high
    for out, stack in (
        (left, [row_high, row_high, row_low]),
        (right, [col_high, col_low, col_high]),
        (thin, [row_high, row_low]),
    ):
        spare = out.shape[0] - len(stack) * seqs
        if spare:
            stack.append(jnp.zeros((spare, out.shape[1]), jnp.float32))
        out[...] = jnp.concatenate(stack).astype(jnp.bfloat16)
    col[...] = column


def spread(me, gathered, dp, mp, rows_here, cols_here):
    seqs = gathered.shape[0]
    deep = -(-3 * seqs // 16) * 16
    thin = -(-2 * seqs // LANES) * LANES
    return pl.pallas_call(
        functools.partial(spread_kernel, seqs, dp, mp),
        out_shape=[
            jax.ShapeDtypeStruct((deep, rows_here), jnp.bfloat16),
            jax.ShapeDtypeStruct((deep, cols_here), jnp.bfloat16),
            jax.ShapeDtypeStruct((thin, rows_here), jnp.bfloat16),
            jax.ShapeDtypeStruct((seqs, cols_here), jnp.float32),
        ],
        in_specs=[
            pl.BlockSpec(memory_space=pltpu.SMEM),
            pl.BlockSpec(memory_space=pltpu.VMEM),
        ],
        scratch_shapes=[
            pltpu.VMEM((seqs, rows_here), jnp.float32),
            pltpu.VMEM((seqs, cols_here), jnp.float32),
        ],
        compiler_params=params(),
        cost_estimate=cost(0, 1000000),
    )(me, gathered)


def update_kernel(scale, gram, left, right, out):
    out[...] = gram[...] + dot(left[...], right[...], TN) * scale


def update(scale, gram, left, right):
    rows, cols = gram.shape
    tile = min(rows, 128)
    deep = left.shape[0]
    return pl.pallas_call(
        functools.partial(update_kernel, scale),
        out_shape=jax.ShapeDtypeStruct(gram.shape, jnp.float32),
        grid=(rows // tile,),
        in_specs=[
            pl.BlockSpec((tile, cols), lambda i: (i, 0)),
            pl.BlockSpec((deep, tile), lambda i: (0, i)),
            pl.BlockSpec((deep, cols), lambda i: (0, 0)),
        ],
        out_specs=pl.BlockSpec((tile, cols), lambda i: (i, 0)),
        compiler_params=params(),
        cost_estimate=cost(2 * rows * cols * deep, 8 * rows * cols),
    )(gram, left, right)


def product_kernel(n_low, has_more, has_recv, me, can, gram, *rest):
    rest = list(rest)
    more = rest.pop(0) if has_more else None
    recv = rest.pop(0) if has_recv else None
    low = rest.pop(0)
    keep = rest.pop(0) if rest[1:] else None
    gram_low = rest.pop(0)
    step = pl.program_id(0)
    width = gram.shape[1]

    @pl.when(step == 0)
    def _():
        gram_low[...] = gram[...].astype(jnp.bfloat16)

    rows = can[...].reshape(-1, can.shape[-1])
    value = dot(rows, gram_low[...], (((1,), (0,)), ((), ())))
    if has_more:
        value = jnp.concatenate([value, dot(rows, more[...], NT)], axis=1)
    if has_recv:
        value = value + recv[...].astype(jnp.float32)
    if keep is None:
        low[...] = value.astype(jnp.bfloat16)
    else:

        @pl.when(step < n_low)
        def _():
            low[...] = value.astype(jnp.bfloat16)

        @pl.when(step >= n_low)
        def _():
            keep[...] = value


def product(where, me, can, gram, more, recv, piece, width, first, count, n_low, chunk):
    units, unit, depth = can.shape
    per = chunk // unit
    full = width + (more.shape[0] if more is not None else 0)
    in_specs = [
        pl.BlockSpec((per, unit, depth), lambda i, me: (where(me[0], first + i), 0, 0)),
        pl.BlockSpec((depth, width), lambda i, me: (0, piece)),
    ]
    args = [can, gram]
    if more is not None:
        in_specs.append(pl.BlockSpec(more.shape, lambda i, me: (0, 0)))
        args.append(more)
    if recv is not None:
        in_specs.append(pl.BlockSpec((chunk, full), lambda i, me: (i, 0)))
        args.append(recv)
    out_shape = [jax.ShapeDtypeStruct((n_low * chunk, full), jnp.bfloat16)]
    out_specs = [pl.BlockSpec((chunk, full), lambda i, me: (jnp.minimum(i, n_low - 1), 0))]
    if count > n_low:
        out_shape.append(jax.ShapeDtypeStruct(((count - n_low) * chunk, full), jnp.float32))
        out_specs.append(
            pl.BlockSpec((chunk, full), lambda i, me: (jnp.maximum(i - n_low, 0), 0))
        )
    return pl.pallas_call(
        functools.partial(product_kernel, n_low, more is not None, recv is not None),
        out_shape=out_shape,
        grid_spec=pltpu.PrefetchScalarGridSpec(
            num_scalar_prefetch=1,
            grid=(count,),
            in_specs=in_specs,
            out_specs=out_specs,
            scratch_shapes=[pltpu.VMEM((depth, width), jnp.bfloat16)],
        ),
        compiler_params=params(),
        cost_estimate=cost(2 * count * chunk * full * depth, 4 * depth * width + 2 * count * chunk * (depth + full)),
    )(me, *args)


def finish_kernel(seqs, scale, norm, pieces, *refs):
    own, (col, mapped, scores) = refs[:-3], refs[-3:]
    column = col[...]
    values = []
    for at in range(len(own) // pieces):
        terms = own[at * pieces : (at + 1) * pieces]
        value = terms[0][...]
        for term in terms[1:]:
            value = value + term[...].astype(jnp.float32)
        values.append(value)
    width = values[0].shape[1]
    last = values[-1]
    thin = last[:, width:]
    thin = (thin[:, :seqs] + thin[:, seqs : 2 * seqs]) * scale
    values[-1] = last[:, :width]
    whole = jnp.concatenate(values, axis=1)
    whole = whole + dot(thin, column, (((1,), (0,)), ((), ())), lax.Precision.HIGHEST)
    whole = whole * norm
    mapped[...] = whole.astype(jnp.bfloat16)
    scores[...] = dot(column, whole, NT, lax.Precision.HIGHEST) * norm


def finish(scale, norm, kept, col, chunk):
    seqs, cols = col.shape
    in_specs, args = [], []
    for keep, arrived in kept:
        in_specs.append(pl.BlockSpec((chunk, keep.shape[1]), lambda i, n=keep.shape[0]: (n // chunk - 1, 0)))
        args.append(keep)
        for array in arrived:
            in_specs.append(pl.BlockSpec((chunk, array.shape[1]), lambda i, n=array.shape[0]: (n // chunk - 1, 0)))
            args.append(array)
    in_specs.append(pl.BlockSpec((seqs, cols), lambda i: (0, 0)))
    return pl.pallas_call(
        functools.partial(finish_kernel, seqs, scale, norm, len(args) // len(kept)),
        out_shape=[
            jax.ShapeDtypeStruct((chunk, cols), jnp.bfloat16),
            jax.ShapeDtypeStruct((seqs, chunk), jnp.float32),
        ],
        grid=(1,),
        in_specs=in_specs,
        out_specs=[
            pl.BlockSpec((chunk, cols), lambda i: (0, 0)),
            pl.BlockSpec((seqs, chunk), lambda i: (0, 0)),
        ],
        compiler_params=params(),
        cost_estimate=cost(24 * chunk * cols * seqs, 14 * chunk * cols),
    )(*args, col)


def shards(
    sizes,
    up_input,
    gate_pre,
    up_pre,
    grad_hidden,
    grad_output,
    proj_up_in,
    proj_up_out,
    proj_down_in,
    proj_down_out,
    gram,
    canaries,
):
    grp, dp, mp = sizes
    rank = proj_up_in.shape[0]
    seq_len = up_input.shape[1]
    rows_here, cols_here = gram.shape
    features = rows_here * grp * mp
    can_here = canaries.shape[0]
    chunk = can_here * dp // (grp * mp)
    me = lax.axis_index(("grp", "dp", "mp")).astype(jnp.int32).reshape(1)

    direct = can_here >= chunk
    if direct:
        blocks = {0: canaries}
        for bit in bits_of(dp):
            blocks |= {at ^ bit: lax.ppermute(block, "dp", pairs(dp, bit)) for at, block in blocks.items()}
        can = jnp.concatenate([blocks[at] for at in range(dp)])
    else:
        can = lax.all_gather(canaries, "dp", axis=0, tiled=True)
    can = can.reshape(-1, chunk, canaries.shape[1])

    codes = [0]
    halvings = [("grp", grp, bit, bit * mp) for bit in bits_of(grp)]
    halvings += [("mp", mp, bit, bit) for bit in reversed(bits_of(mp))]
    for _, _, _, code in reversed(halvings):
        codes = [at | code for at in codes] + codes

    def where(me, at):
        code = 0
        for place, value in enumerate(codes):
            code = jnp.where(at == place, value, code) if place else jnp.int32(value)
        target = ((me // (dp * mp)) * mp + me % mp) ^ code
        if not direct:
            return target
        row = target * chunk
        block = (row // can_here) ^ ((me // mp) % dp)
        return (block * can_here + row % can_here) // chunk

    parts = project_all(
        mp, me, up_input, gate_pre, up_pre, grad_hidden, grad_output,
        proj_up_in, proj_up_out, proj_down_in, proj_down_out,
    )
    parts = [parts[0]] + [lax.ppermute(parts[at], "mp", pairs(mp, at)) for at in range(1, mp)]
    row = feature_rows(1.0 / math.sqrt(seq_len), rank, parts)
    for bit in reversed(bits_of(mp)):
        row = row + lax.ppermute(row, "mp", pairs(mp, bit))
    gathered = row[None]
    for axis, size in (("grp", grp), ("dp", dp)):
        for bit in bits_of(size):
            gathered = jnp.concatenate([gathered, lax.ppermute(gathered, axis, pairs(size, bit))])
    left, right, thin, col = spread(me, gathered, dp, mp, rows_here, cols_here)
    seqs = gathered.shape[0]
    gram_new = update(1.0 / seqs, gram, left, right)

    width = max(LANES, cols_here // 4)
    n_pieces = cols_here // width
    total = grp * mp
    kept = []
    for piece in range(n_pieces):
        more = thin if piece == n_pieces - 1 else None
        take = functools.partial(product, where, me, can, gram, more)
        axis, size, bit, _ = halvings[0]
        (low,) = take(None, piece, width, 0, total // 2, total // 2, chunk)
        recv = lax.ppermute(low, axis, pairs(size, bit))
        left_over = total // 2
        low, keep = take(recv, piece, width, total // 2, left_over, left_over // 2, chunk)
        arrived = []
        for at, (axis, size, bit, _) in enumerate(halvings[1:]):
            recv = lax.ppermute(low, axis, pairs(size, bit))
            arrived.append(recv)
            left_over //= 2
            if left_over > 1:
                half = (left_over // 2) * chunk
                low = keep[:half]
                for array in arrived:
                    low = low + array[-left_over * chunk :][:half].astype(jnp.float32)
                low = low.astype(jnp.bfloat16)
                keep = keep[half:]
        kept.append((keep, arrived))
    norm = 1.0 / math.sqrt(features)
    mapped, scores = finish(1.0 / seqs, norm, kept, col, chunk)
    for bit in bits_of(dp):
        scores = scores + lax.ppermute(scores, "dp", pairs(dp, bit))
    return gram_new, mapped, scores


def solution(mesh):
    sizes = tuple(mesh.shape[name] for name in ("grp", "dp", "mp"))
    wide = P(("grp", "dp"), None, "mp")
    return jax.shard_map(
        functools.partial(shards, sizes),
        mesh=mesh,
        in_specs=(wide, wide, wide, wide, wide)
        + (P(None, "mp"),) * 4
        + (P(("grp", "mp"), "dp"), P("dp", ("grp", "mp"))),
        out_specs=(P(("grp", "mp"), "dp"), P(("grp", "mp"), "dp"), P(None, ("grp", "mp"))),
        check_vma=False,
    )
```

time: 263 us -> 155 us (0.59)
  waiting for transfers between devices: 190 us -> 75.2 us
  Pallas kernels: 0 us -> 43.2 us
  matrix products: 36.5 us -> 0 us
  starting transfers between devices: 0.12 us -> 24.6 us
  blocking collectives: 16.8 us -> 0 us
  between operations: 15.6 us -> 0.86 us
  local copies, waits for them, and re-layouts: 2.22 us -> 8.93 us
    reduce_scatter x1 -> x0, waiting for transfers between devices: 148 us -> none  [shards(): lax.psum_scatter(jnp.dot(gathered, gram_low, preferred_element_type=jnp.f...]
    ppermute x0 -> x25, waiting for transfers between devices: none -> 75.2 us  [the longest x12 53.2 us: shards(): recv = lax.ppermute(low, axis, pairs(size, bit))]
    pallas_call x0 -> x13, Pallas kernels: none -> 43.2 us  [the longest x8 25.6 us: product(): pl.pallas_call(functools.partial(product_kernel, n_low, more is not None,...]
    psum x1 -> x0, waiting for transfers between devices: 41.2 us -> none  [shards(): lax.psum((project(up_input[0], proj_up_in), project(grad_up, proj_up_out)...]
    dot_general x9 -> x0, matrix products: 36.5 us -> none  [the longest x1 11.8 us: shards(): jnp.dot(gathered, gram_low, preferred_element_type=jnp.float32)]
    ppermute x0 -> x25, starting transfers between devices: none -> 24.6 us  [the longest x12 12.7 us: shards(): recv = lax.ppermute(low, axis, pairs(size, bit))]
    all_gather x1 -> x0, blocking collectives: 9.33 us -> none  [shards(): feature_rows = lax.all_gather(own_row, ('grp', 'dp'), axis=0, tiled=True)]
    psum x1 -> x0, blocking collectives: 7.42 us -> none  [shards(): lax.psum(jnp.dot(right_block, mapped_share.T, precision=lax.Precision.HIG...]
  transfers between devices with their start and end apart: 3 -> 25, of which waited for: 2 -> 12; matrix products, arithmetic and copies ran while one was open for 5% -> 0% of each run, Pallas kernels for 0% -> 26%
where the time goes in v1:
time: 155 us; the launch traced here: 154 us
  waiting for transfers between devices  75.2 us (49%)
  Pallas kernels  43.2 us (28%)
  starting transfers between devices  24.6 us (16%)
  local copies, waits for them, and re-layouts  8.93 us (6%)
    ppermute x12, waiting for transfers between devices, shards(): recv = lax.ppermute(low, axis, pairs(size, bit))  53.2 us
    pallas_call x8, Pallas kernels, product(): pl.pallas_call(functools.partial(product_kernel, n_low, more is not None,...  25.6 us
    ppermute x12, starting transfers between devices, shards(): recv = lax.ppermute(low, axis, pairs(size, bit))  12.7 us
    pallas_call x1, Pallas kernels, update(): pl.pallas_call(functools.partial(update_kernel, scale), out_shape=jax.Sha...  9.85 us
    unnamed x18, local copies, waits for them, and re-layouts  8.93 us
    ppermute x2, waiting for transfers between devices, shards(): row = row + lax.ppermute(row, 'mp', pairs(mp, bit))  6.89 us
    ppermute x3, waiting for transfers between devices, shards(): lax.ppermute(gathered, axis, pairs(size, bit))  6.19 us
    ppermute x3, waiting for transfers between devices, shards(): lax.ppermute(parts[at], 'mp', pairs(mp, at))  5.84 us
  transfers between devices with their start and end apart: 25, of which 12 were waited for; matrix products, arithmetic and copies ran while one was open for 0% of the time, Pallas kernels for 26%

profile of v1, /device:TPU:0, one launch (start us, length us, event | category | flops | bytes accessed | tf_op | source)
XLA Modules:
  0.0 153.8 jit_solution(13232386724423947143)
XLA Ops:
  0.6 3.0 %collective-permute-start.9 = (bf16[256,1024]{1,0:T(8,128)(2,1)}, bf16[256,1024]{1,0:T(8,128)(2,1)S(1)}, u32[]{:S(2)}, u32[]{:S(2)}) collective-permute-start(bf16[256,1024]{1,0:T(8,128)(2,1)} %param.21), channel_id=1, source_target_pairs={{0,8},{4,12},{8,0},{12,4},{1,9},{5,13},{9,1},{13,5},{2,10},{6,14},... | collective-permute-start | bytes 1572872 | tf_op jit(solution)/shard_map/ppermute | solution.py:352
  3.7 1.5 copy-done
  5.2 1.5 copy-done.1
  12.6 4.6 %shard_map.130 = (f32[64,256]{1,0:T(8,128)S(1)}, f32[64,256]{1,0:T(8,128)S(1)}, f32[64,256]{1,0:T(8,128)S(1)}, f32[64,256]{1,0:T(8,128)S(1)}) custom-call(s32[1]{0:T(128)} %bitcast.me, bf16[1,256,1024]{2,1,0:T(8,128)(2,1)S(1)} %copy-done.2, bf16[1,256,3584]{2,1,0:T(8,128)(2,1)S(1)} %copy-done, bf16[1,256,3584]{2,1,0:T(8,128)(2,1)S(1)} %copy-done.1, ...), custom_call_target="tpu_custom_call" | custom-call | flops 301989888 | bytes 6553600 | tf_op jit(solution)/shard_map/pallas_call | solution.py:78
  17.2 1.6 %collective-permute-start = (f32[64,256]{1,0:T(8,128)S(1)}, f32[64,256]{1,0:T(8,128)S(1)}, u32[]{:S(2)}, u32[]{:S(2)}) collective-permute-start(f32[64,256]{1,0:T(8,128)S(1)} %get-tuple-element.22), channel_id=1, source_target_pairs={{0,1},{1,0},{2,3},{3,2},{4,5},{5,4},{6,7},{7,6},{8,9},{9,8},{10,11... | collective-permute-start | bytes 196616 | tf_op jit(solution)/shard_map/ppermute | solution.py:379
  18.8 2.6 %collective-permute-start.1 = (f32[64,256]{1,0:T(8,128)S(1)}, f32[64,256]{1,0:T(8,128)S(1)}, u32[]{:S(2)}, u32[]{:S(2)}) collective-permute-start(f32[64,256]{1,0:T(8,128)S(1)} %get-tuple-element.23), channel_id=1, source_target_pairs={{0,2},{1,3},{2,0},{3,1},{4,6},{5,7},{6,4},{7,5},{8,10},{9,11},{10,... | collective-permute-start | bytes 196616 | tf_op jit(solution)/shard_map/ppermute | solution.py:379
  21.7 4.2 %collective-permute-done.1.refs_2_ = f32[64,256]{1,0:T(8,128)S(1)} collective-permute-done((f32[64,256]{1,0:T(8,128)S(1)}, f32[64,256]{1,0:T(8,128)S(1)}, u32[]{:S(2)}, u32[]{:S(2)}) %collective-permute-start.1) | collective-permute-done | bytes 65568 | tf_op jit(solution)/shard_map/ppermute | solution.py:379
  25.8 1.7 %collective-permute-done.2.refs_3_ = f32[64,256]{1,0:T(8,128)S(1)} collective-permute-done((f32[64,256]{1,0:T(8,128)S(1)}, f32[64,256]{1,0:T(8,128)S(1)}, u32[]{:S(2)}, u32[]{:S(2)}) %collective-permute-start.2) | collective-permute-done | bytes 65568 | tf_op jit(solution)/shard_map/ppermute | solution.py:379
  28.0 3.9 %collective-permute-done.3 = f32[64,128]{1,0:T(8,128)S(1)} collective-permute-done((f32[64,128]{1,0:T(8,128)S(1)}, f32[64,128]{1,0:T(8,128)S(1)}, u32[]{:S(2)}, u32[]{:S(2)}) %collective-permute-start.3) | collective-permute-done | bytes 32800 | tf_op jit(solution)/shard_map/ppermute | solution.py:382
  33.7 3.0 %collective-permute-done.4 = f32[64,128]{1,0:T(8,128)S(1)} collective-permute-done((f32[64,128]{1,0:T(8,128)S(1)}, f32[64,128]{1,0:T(8,128)S(1)}, u32[]{:S(2)}, u32[]{:S(2)}) %collective-permute-start.4) | collective-permute-done | bytes 32800 | tf_op jit(solution)/shard_map/ppermute | solution.py:382
  38.2 2.4 %collective-permute-done.5 = f32[1,64,128]{2,1,0:T(8,128)S(1)} collective-permute-done((f32[1,64,128]{2,1,0:T(8,128)S(1)}, f32[1,64,128]{2,1,0:T(8,128)S(1)}, u32[]{:S(2)}, u32[]{:S(2)}) %collective-permute-start.5) | collective-permute-done | bytes 32800 | tf_op jit(solution)/shard_map/ppermute | solution.py:386
  41.1 3.8 %collective-permute-done.6 = f32[2,64,128]{2,1,0:T(8,128)S(1)} collective-permute-done((f32[2,64,128]{2,1,0:T(8,128)S(1)}, f32[2,64,128]{2,1,0:T(8,128)S(1)}, u32[]{:S(2)}, u32[]{:S(2)}) %collective-permute-start.6) | collective-permute-done | bytes 65568 | tf_op jit(solution)/shard_map/ppermute | solution.py:386
  45.2 3.1 %shard_map.134 = bf16[512,512]{1,0:T(8,128)(2,1)S(1)} custom-call(s32[1]{0:T(128)} %bitcast.me, bf16[8,128,1024]{2,1,0:T(8,128)(2,1)S(1)} %bitcast.4, f32[1024,2048]{1,0:T(8,128)} %gram.17), custom_call_target="tpu_custom_call" | custom-call | flops 536870912 | bytes 3670016 | tf_op jit(solution)/shard_map/pallas_call | solution.py:261
  48.3 1.6 %collective-permute-start.11 = (bf16[512,512]{1,0:T(8,128)(2,1)S(1)}, bf16[512,512]{1,0:T(8,128)(2,1)S(1)}, u32[]{:S(2)}, u32[]{:S(2)}) collective-permute-start(bf16[512,512]{1,0:T(8,128)(2,1)S(1)} %shard_map.134), channel_id=1, source_target_pairs={{0,16},{16,0},{1,17},{17,1},{2,18},{18,2},{3,19},{19,3},{4,20},{20... | collective-permute-start | bytes 1572872 | tf_op jit(solution)/shard_map/ppermute | solution.py:400
  50.0 3.4 %shard_map.140 = bf16[512,640]{1,0:T(8,128)(2,1)S(1)} custom-call(s32[1]{0:T(128)} %bitcast.me, bf16[8,128,1024]{2,1,0:T(8,128)(2,1)S(1)} %bitcast.5, f32[1024,2048]{1,0:T(8,128)} %gram.17, bf16[128,1024]{1,0:T(8,128)(2,1)S(1)} %get-tuple-element.33.rest_0_), custom_call_target="tpu_custom_call" | custom-call | flops 671088640 | bytes 3801088 | tf_op jit(solution)/shard_map/pallas_call | solution.py:261
  54.0 3.1 %shard_map.136 = bf16[512,512]{1,0:T(8,128)(2,1)S(1)} custom-call(s32[1]{0:T(128)} %bitcast.me, bf16[8,128,1024]{2,1,0:T(8,128)(2,1)S(1)} %bitcast.6, f32[1024,2048]{1,0:T(8,128)} %gram.17), custom_call_target="tpu_custom_call" | custom-call | flops 536870912 | bytes 3670016 | tf_op jit(solution)/shard_map/pallas_call | solution.py:261
  57.1 1.6 %collective-permute-start.14 = (bf16[512,512]{1,0:T(8,128)(2,1)S(1)}, bf16[512,512]{1,0:T(8,128)(2,1)S(1)}, u32[]{:S(2)}, u32[]{:S(2)}) collective-permute-start(bf16[512,512]{1,0:T(8,128)(2,1)S(1)} %shard_map.136), channel_id=1, source_target_pairs={{0,16},{16,0},{1,17},{17,1},{2,18},{18,2},{3,19},{19,3},{4,20},{20... | collective-permute-start | bytes 1572872 | tf_op jit(solution)/shard_map/ppermute | solution.py:400
  58.7 3.1 %shard_map.138 = bf16[512,512]{1,0:T(8,128)(2,1)S(1)} custom-call(s32[1]{0:T(128)} %bitcast.me, bf16[8,128,1024]{2,1,0:T(8,128)(2,1)S(1)} %bitcast.7, f32[1024,2048]{1,0:T(8,128)} %gram.17), custom_call_target="tpu_custom_call" | custom-call | flops 536870912 | bytes 3670016 | tf_op jit(solution)/shard_map/pallas_call | solution.py:261
  63.1 3.2 %shard_map.135 = (bf16[256,512]{1,0:T(8,128)(2,1)S(1)}, f32[256,512]{1,0:T(8,128)S(1)}) custom-call(s32[1]{0:T(128)} %bitcast.me, bf16[8,128,1024]{2,1,0:T(8,128)(2,1)S(1)} %bitcast.8, f32[1024,2048]{1,0:T(8,128)} %gram.17, bf16[512,512]{1,0:T(8,128)(2,1)S(1)} %collective-permute-done.11.rest_0_), custom_call_target="tpu_custom_call" | custom-call | flops 536870912 | bytes 3670016 | tf_op jit(solution)/shard_map/pallas_call | solution.py:261
  66.4 22.0 %collective-permute-done.14.rest_0_ = bf16[512,512]{1,0:T(8,128)(2,1)S(1)} collective-permute-done((bf16[512,512]{1,0:T(8,128)(2,1)S(1)}, bf16[512,512]{1,0:T(8,128)(2,1)S(1)}, u32[]{:S(2)}, u32[]{:S(2)}) %collective-permute-start.14) | collective-permute-done | bytes 524320 | tf_op jit(solution)/shard_map/ppermute | solution.py:400
  88.4 3.2 %shard_map.137 = (bf16[256,512]{1,0:T(8,128)(2,1)S(1)}, f32[256,512]{1,0:T(8,128)S(1)}) custom-call(s32[1]{0:T(128)} %bitcast.me, bf16[8,128,1024]{2,1,0:T(8,128)(2,1)S(1)} %bitcast.9, f32[1024,2048]{1,0:T(8,128)} %gram.17, bf16[512,512]{1,0:T(8,128)(2,1)S(1)} %collective-permute-done.14.rest_0_), custom_call_target="tpu_custom_call" | custom-call | flops 536870912 | bytes 3670016 | tf_op jit(solution)/shard_map/pallas_call | solution.py:261
  91.6 7.6 %collective-permute-done.17.rest_0_ = bf16[512,512]{1,0:T(8,128)(2,1)S(1)} collective-permute-done((bf16[512,512]{1,0:T(8,128)(2,1)S(1)}, bf16[512,512]{1,0:T(8,128)(2,1)S(1)}, u32[]{:S(2)}, u32[]{:S(2)}) %collective-permute-start.17) | collective-permute-done | bytes 524320 | tf_op jit(solution)/shard_map/ppermute | solution.py:400
  99.2 3.2 %shard_map.139 = (bf16[256,512]{1,0:T(8,128)(2,1)S(1)}, f32[256,512]{1,0:T(8,128)S(1)}) custom-call(s32[1]{0:T(128)} %bitcast.me, bf16[8,128,1024]{2,1,0:T(8,128)(2,1)S(1)} %bitcast.10, f32[1024,2048]{1,0:T(8,128)} %gram.17, bf16[512,512]{1,0:T(8,128)(2,1)S(1)} %collective-permute-done.17.rest_0_), custom_call_target="tpu_custom_call" | custom-call | flops 536870912 | bytes 3670016 | tf_op jit(solution)/shard_map/pallas_call | solution.py:261
  102.5 3.5 %shard_map.141 = (bf16[256,640]{1,0:T(8,128)(2,1)S(1)}, f32[256,640]{1,0:T(8,128)S(1)}) custom-call(s32[1]{0:T(128)} %bitcast.me, bf16[8,128,1024]{2,1,0:T(8,128)(2,1)S(1)} %bitcast.11, f32[1024,2048]{1,0:T(8,128)} %gram.17, bf16[128,1024]{1,0:T(8,128)(2,1)S(1)} %get-tuple-element.33.rest_0_, bf16[512,640]{1,0:T(8,128)(2,1)S(1)} %collective-permute-done.20.rest_1_), custom_call_target="tpu_custom_call" | custom-call | flops 671088640 | bytes 3801088 | tf_op jit(solution)/shard_map/pallas_call | solution.py:261
  105.9 2.0 %collective-permute-start.21 = (bf16[256,640]{1,0:T(8,128)(2,1)S(1)}, bf16[256,640]{1,0:T(8,128)(2,1)S(1)}, u32[]{:S(2)}, u32[]{:S(2)}) collective-permute-start(bf16[256,640]{1,0:T(8,128)(2,1)S(1)} %get-tuple-element.35), channel_id=1, source_target_pairs={{0,1},{1,0},{2,3},{3,2},{4,5},{5,4},{6,7},{7,6},{8,9},{9,8},{10,11... | collective-permute-start | bytes 983048 | tf_op jit(solution)/shard_map/ppermute | solution.py:405
  109.4 1.7 %collective-permute-start.16 = (bf16[128,512]{1,0:T(8,128)(2,1)S(1)}, bf16[128,512]{1,0:T(8,128)(2,1)S(1)}, u32[]{:S(2)}, u32[]{:S(2)}) collective-permute-start(bf16[128,512]{1,0:T(8,128)(2,1)S(1)} %get-tuple-element.43), channel_id=1, source_target_pairs={{0,2},{1,3},{2,0},{3,1},{4,6},{5,7},{6,4},{7,5},{8,10},{9,11},{10,... | collective-permute-start | bytes 393224 | tf_op jit(solution)/shard_map/ppermute | solution.py:405
  111.1 11.9 %collective-permute-done.21.refs_10_ = bf16[256,640]{1,0:T(8,128)(2,1)S(1)} collective-permute-done((bf16[256,640]{1,0:T(8,128)(2,1)S(1)}, bf16[256,640]{1,0:T(8,128)(2,1)S(1)}, u32[]{:S(2)}, u32[]{:S(2)}) %collective-permute-start.21) | collective-permute-done | bytes 327712 | tf_op jit(solution)/shard_map/ppermute | solution.py:405
  123.2 3.0 %collective-permute-start.19 = (bf16[128,512]{1,0:T(8,128)(2,1)S(1)}, bf16[128,512]{1,0:T(8,128)(2,1)S(1)}, u32[]{:S(2)}, u32[]{:S(2)}) collective-permute-start(bf16[128,512]{1,0:T(8,128)(2,1)S(1)} %get-tuple-element.41), channel_id=1, source_target_pairs={{0,2},{1,3},{2,0},{3,1},{4,6},{5,7},{6,4},{7,5},{8,10},{9,11},{10,... | collective-permute-start | bytes 393224 | tf_op jit(solution)/shard_map/ppermute | solution.py:405
  126.2 11.0 %collective-permute-done.19.refs_8_ = bf16[128,512]{1,0:T(8,128)(2,1)S(1)} collective-permute-done((bf16[128,512]{1,0:T(8,128)(2,1)S(1)}, bf16[128,512]{1,0:T(8,128)(2,1)S(1)}, u32[]{:S(2)}, u32[]{:S(2)}) %collective-permute-start.19) | collective-permute-done | bytes 131104 | tf_op jit(solution)/shard_map/ppermute | solution.py:405
  137.2 2.6 %shard_map.142 = (bf16[128,2048]{1,0:T(8,128)(2,1)}, f32[8,128]{1,0:T(8,128)S(1)}) custom-call(f32[128,512]{1,0:T(8,128)S(1)} %get-tuple-element.46.refs_0_, bf16[256,512]{1,0:T(8,128)(2,1)S(1)} %collective-permute-done.12.refs_1_, bf16[128,512]{1,0:T(8,128)(2,1)S(1)} %collective-permute-done.13.refs_2_, f32[128,512]{1,0:T(8,128)S(1)} %get-tuple-element.44.refs_3_, ...), custom_call_target="tpu_custom_call" | custom-call | flops 50331648 | bytes 3670016 | tf_op jit(solution)/shard_map/pallas_call | solution.py:308
  140.2 3.1 %collective-permute-done.23 = f32[8,128]{1,0:T(8,128)S(1)} collective-permute-done((f32[8,128]{1,0:T(8,128)S(1)}, f32[8,128]{1,0:T(8,128)S(1)}, u32[]{:S(2)}, u32[]{:S(2)}) %collective-permute-start.23) | collective-permute-done | bytes 4128 | tf_op jit(solution)/shard_map/ppermute | solution.py:419
  143.4 9.8 %shard_map.133 = f32[1024,2048]{1,0:T(8,128)} custom-call(f32[1024,2048]{1,0:T(8,128)} %gram.17, bf16[32,1024]{1,0:T(8,128)(2,1)S(1)} %get-tuple-element.25.left, bf16[32,2048]{1,0:T(8,128)(2,1)S(1)} %get-tuple-element.26.right), custom_call_target="tpu_custom_call" | custom-call | flops 134217728 | bytes 16777216 | tf_op jit(solution)/shard_map/pallas_call | solution.py:191
  (61 shorter events, 15.7 us)
Async XLA Ops:
  0.6 32.6 %collective-permute-start.9 = (bf16[256,1024]{1,0:T(8,128)(2,1)}, bf16[256,1024]{1,0:T(8,128)(2,1)S(1)}, u32[]{:S(2)}, u32[]{:S(2)}) collective-permute-start(bf16[256,1024]{1,0:T(8,128)(2,1)} %param.21), channel_id=1, source_target_pairs={{0,8},{4,12},{8,0},{12,4},{1,9},{5,13},{9,1},{13,5},{2,10},{6,14},... | collective-permute-start | bytes 1572872 | tf_op jit(solution)/shard_map/ppermute | solution.py:352
  3.7 1.5 copy-start
  5.2 1.5 copy-start.1
  6.7 1.0 copy-start.2
  7.7 1.0 copy-start.3
  8.8 1.0 copy-start.4
  9.8 1.0 copy-start.5
  12.6 20.6 %copy-start.8 = (bf16[256,1024]{1,0:T(8,128)(2,1)S(1)}, bf16[256,1024]{1,0:T(8,128)(2,1)}, u32[]{:S(2)}) copy-start(bf16[256,1024]{1,0:T(8,128)(2,1)} %param.21) | copy-start | bytes 1572868
  17.2 4.5 %collective-permute-start = (f32[64,256]{1,0:T(8,128)S(1)}, f32[64,256]{1,0:T(8,128)S(1)}, u32[]{:S(2)}, u32[]{:S(2)}) collective-permute-start(f32[64,256]{1,0:T(8,128)S(1)} %get-tuple-element.22), channel_id=1, source_target_pairs={{0,1},{1,0},{2,3},{3,2},{4,5},{5,4},{6,7},{7,6},{8,9},{9,8},{10,11... | collective-permute-start | bytes 196616 | tf_op jit(solution)/shard_map/ppermute | solution.py:379
  18.8 7.0 %collective-permute-start.1 = (f32[64,256]{1,0:T(8,128)S(1)}, f32[64,256]{1,0:T(8,128)S(1)}, u32[]{:S(2)}, u32[]{:S(2)}) collective-permute-start(f32[64,256]{1,0:T(8,128)S(1)} %get-tuple-element.23), channel_id=1, source_target_pairs={{0,2},{1,3},{2,0},{3,1},{4,6},{5,7},{6,4},{7,5},{8,10},{9,11},{10,... | collective-permute-start | bytes 196616 | tf_op jit(solution)/shard_map/ppermute | solution.py:379
  21.4 6.1 %collective-permute-start.2 = (f32[64,256]{1,0:T(8,128)S(1)}, f32[64,256]{1,0:T(8,128)S(1)}, u32[]{:S(2)}, u32[]{:S(2)}) collective-permute-start(f32[64,256]{1,0:T(8,128)S(1)} %get-tuple-element.24), channel_id=1, source_target_pairs={{0,3},{1,2},{2,1},{3,0},{4,7},{5,6},{6,5},{7,4},{8,11},{9,10},{10,... | collective-permute-start | bytes 196616 | tf_op jit(solution)/shard_map/ppermute | solution.py:379
  27.9 4.0 %collective-permute-start.3 = (f32[64,128]{1,0:T(8,128)S(1)}, f32[64,128]{1,0:T(8,128)S(1)}, u32[]{:S(2)}, u32[]{:S(2)}) collective-permute-start(f32[64,128]{1,0:T(8,128)S(1)} %shard_map.131), channel_id=1, source_target_pairs={{0,1},{1,0},{2,3},{3,2},{4,5},{5,4},{6,7},{7,6},{8,9},{9,8},{10,11... | collective-permute-start | bytes 98312 | tf_op jit(solution)/shard_map/ppermute | solution.py:382
  31.9 4.8 %collective-permute-start.4 = (f32[64,128]{1,0:T(8,128)S(1)}, f32[64,128]{1,0:T(8,128)S(1)}, u32[]{:S(2)}, u32[]{:S(2)}) collective-permute-start(f32[64,128]{1,0:T(8,128)S(1)} %add.32), channel_id=1, source_target_pairs={{0,2},{1,3},{2,0},{3,1},{4,6},{5,7},{6,4},{7,5},{8,10},{9,11},{10,... | collective-permute-start | bytes 98312 | tf_op jit(solution)/shard_map/ppermute | solution.py:382
  33.2 11.8 %collective-permute-start.8 = (bf16[256,1024]{1,0:T(8,128)(2,1)S(1)}, bf16[256,1024]{1,0:T(8,128)(2,1)S(1)}, u32[]{:S(2)}, u32[]{:S(2)}) collective-permute-start(bf16[256,1024]{1,0:T(8,128)(2,1)S(1)} %copy-done.8), channel_id=1, source_target_pairs={{0,4},{4,0},{8,12},{12,8},{1,5},{5,1},{9,13},{13,9},{2,6},{6,2},{1... | collective-permute-start | bytes 1572872 | tf_op jit(solution)/shard_map/ppermute | solution.py:352
  33.2 11.8 %collective-permute-start.10 = (bf16[256,1024]{1,0:T(8,128)(2,1)S(1)}, bf16[256,1024]{1,0:T(8,128)(2,1)S(1)}, u32[]{:S(2)}, u32[]{:S(2)}) collective-permute-start(bf16[256,1024]{1,0:T(8,128)(2,1)S(1)} %collective-permute-done.9), channel_id=1, source_target_pairs={{0,4},{4,0},{8,12},{12,8},{1,5},{5,1},{9,13},{13,9},{2,6},{6,2},{1... | collective-permute-start | bytes 1572872 | tf_op jit(solution)/shard_map/ppermute | solution.py:352
  36.7 3.9 %collective-permute-start.5 = (f32[1,64,128]{2,1,0:T(8,128)S(1)}, f32[1,64,128]{2,1,0:T(8,128)S(1)}, u32[]{:S(2)}, u32[]{:S(2)}) collective-permute-start(f32[1,64,128]{2,1,0:T(8,128)S(1)} %add_bitcast_fusion), channel_id=1, source_target_pairs={{0,16},{16,0},{1,17},{17,1},{2,18},{18,2},{3,19},{19,3},{4,20},{20... | collective-permute-start | bytes 98312 | tf_op jit(solution)/shard_map/ppermute | solution.py:386
  40.6 4.3 %collective-permute-start.6 = (f32[2,64,128]{2,1,0:T(8,128)S(1)}, f32[2,64,128]{2,1,0:T(8,128)S(1)}, u32[]{:S(2)}, u32[]{:S(2)}) collective-permute-start(f32[2,64,128]{2,1,0:T(8,128)S(1)} %pad_maximum_fusion.3), channel_id=1, source_target_pairs={{0,8},{4,12},{8,0},{12,4},{1,9},{5,13},{9,1},{13,5},{2,10},{6,14},... | collective-permute-start | bytes 196616 | tf_op jit(solution)/shard_map/ppermute | solution.py:386
  44.9 5.0 %collective-permute-start.7 = (f32[4,64,128]{2,1,0:T(8,128)S(1)}, f32[4,64,128]{2,1,0:T(8,128)S(1)}, u32[]{:S(2)}, u32[]{:S(2)}) collective-permute-start(f32[4,64,128]{2,1,0:T(8,128)S(1)} %pad_maximum_fusion.2), channel_id=1, source_target_pairs={{0,4},{4,0},{8,12},{12,8},{1,5},{5,1},{9,13},{13,9},{2,6},{6,2},{1... | collective-permute-start | bytes 393224 | tf_op jit(solution)/shard_map/ppermute | solution.py:386
  48.3 14.8 %collective-permute-start.11 = (bf16[512,512]{1,0:T(8,128)(2,1)S(1)}, bf16[512,512]{1,0:T(8,128)(2,1)S(1)}, u32[]{:S(2)}, u32[]{:S(2)}) collective-permute-start(bf16[512,512]{1,0:T(8,128)(2,1)S(1)} %shard_map.134), channel_id=1, source_target_pairs={{0,16},{16,0},{1,17},{17,1},{2,18},{18,2},{3,19},{19,3},{4,20},{20... | collective-permute-start | bytes 1572872 | tf_op jit(solution)/shard_map/ppermute | solution.py:400
  53.4 49.0 %collective-permute-start.20 = (bf16[512,640]{1,0:T(8,128)(2,1)S(1)}, bf16[512,640]{1,0:T(8,128)(2,1)S(1)}, u32[]{:S(2)}, u32[]{:S(2)}) collective-permute-start(bf16[512,640]{1,0:T(8,128)(2,1)S(1)} %shard_map.140), channel_id=1, source_target_pairs={{0,16},{16,0},{1,17},{17,1},{2,18},{18,2},{3,19},{19,3},{4,20},{20... | collective-permute-start | bytes 1966088 | tf_op jit(solution)/shard_map/ppermute | solution.py:400
  57.1 31.3 %collective-permute-start.14 = (bf16[512,512]{1,0:T(8,128)(2,1)S(1)}, bf16[512,512]{1,0:T(8,128)(2,1)S(1)}, u32[]{:S(2)}, u32[]{:S(2)}) collective-permute-start(bf16[512,512]{1,0:T(8,128)(2,1)S(1)} %shard_map.136), channel_id=1, source_target_pairs={{0,16},{16,0},{1,17},{17,1},{2,18},{18,2},{3,19},{19,3},{4,20},{20... | collective-permute-start | bytes 1572872 | tf_op jit(solution)/shard_map/ppermute | solution.py:400
  61.8 37.4 %collective-permute-start.17 = (bf16[512,512]{1,0:T(8,128)(2,1)S(1)}, bf16[512,512]{1,0:T(8,128)(2,1)S(1)}, u32[]{:S(2)}, u32[]{:S(2)}) collective-permute-start(bf16[512,512]{1,0:T(8,128)(2,1)S(1)} %shard_map.138), channel_id=1, source_target_pairs={{0,16},{16,0},{1,17},{17,1},{2,18},{18,2},{3,19},{19,3},{4,20},{20... | collective-permute-start | bytes 1572872 | tf_op jit(solution)/shard_map/ppermute | solution.py:400
  66.3 41.7 %collective-permute-start.12 = (bf16[256,512]{1,0:T(8,128)(2,1)S(1)}, bf16[256,512]{1,0:T(8,128)(2,1)S(1)}, u32[]{:S(2)}, u32[]{:S(2)}) collective-permute-start(bf16[256,512]{1,0:T(8,128)(2,1)S(1)} %get-tuple-element.28), channel_id=1, source_target_pairs={{0,1},{1,0},{2,3},{3,2},{4,5},{5,4},{6,7},{7,6},{8,9},{9,8},{10,11... | collective-permute-start | bytes 786440 | tf_op jit(solution)/shard_map/ppermute | solution.py:405
  91.6 17.8 %collective-permute-start.15 = (bf16[256,512]{1,0:T(8,128)(2,1)S(1)}, bf16[256,512]{1,0:T(8,128)(2,1)S(1)}, u32[]{:S(2)}, u32[]{:S(2)}) collective-permute-start(bf16[256,512]{1,0:T(8,128)(2,1)S(1)} %get-tuple-element.30), channel_id=1, source_target_pairs={{0,1},{1,0},{2,3},{3,2},{4,5},{5,4},{6,7},{7,6},{8,9},{9,8},{10,11... | collective-permute-start | bytes 786440 | tf_op jit(solution)/shard_map/ppermute | solution.py:405
  102.4 20.7 %collective-permute-start.18 = (bf16[256,512]{1,0:T(8,128)(2,1)S(1)}, bf16[256,512]{1,0:T(8,128)(2,1)S(1)}, u32[]{:S(2)}, u32[]{:S(2)}) collective-permute-start(bf16[256,512]{1,0:T(8,128)(2,1)S(1)} %get-tuple-element.32), channel_id=1, source_target_pairs={{0,1},{1,0},{2,3},{3,2},{4,5},{5,4},{6,7},{7,6},{8,9},{9,8},{10,11... | collective-permute-start | bytes 786440 | tf_op jit(solution)/shard_map/ppermute | solution.py:405
  105.9 17.1 %collective-permute-start.21 = (bf16[256,640]{1,0:T(8,128)(2,1)S(1)}, bf16[256,640]{1,0:T(8,128)(2,1)S(1)}, u32[]{:S(2)}, u32[]{:S(2)}) collective-permute-start(bf16[256,640]{1,0:T(8,128)(2,1)S(1)} %get-tuple-element.35), channel_id=1, source_target_pairs={{0,1},{1,0},{2,3},{3,2},{4,5},{5,4},{6,7},{7,6},{8,9},{9,8},{10,11... | collective-permute-start | bytes 983048 | tf_op jit(solution)/shard_map/ppermute | solution.py:405
  108.0 18.1 %collective-permute-start.13 = (bf16[128,512]{1,0:T(8,128)(2,1)S(1)}, bf16[128,512]{1,0:T(8,128)(2,1)S(1)}, u32[]{:S(2)}, u32[]{:S(2)}) collective-permute-start(bf16[128,512]{1,0:T(8,128)(2,1)S(1)} %get-tuple-element.45), channel_id=1, source_target_pairs={{0,2},{1,3},{2,0},{3,1},{4,6},{5,7},{6,4},{7,5},{8,10},{9,11},{10,... | collective-permute-start | bytes 393224 | tf_op jit(solution)/shard_map/ppermute | solution.py:405
  109.4 16.7 %collective-permute-start.16 = (bf16[128,512]{1,0:T(8,128)(2,1)S(1)}, bf16[128,512]{1,0:T(8,128)(2,1)S(1)}, u32[]{:S(2)}, u32[]{:S(2)}) collective-permute-start(bf16[128,512]{1,0:T(8,128)(2,1)S(1)} %get-tuple-element.43), channel_id=1, source_target_pairs={{0,2},{1,3},{2,0},{3,1},{4,6},{5,7},{6,4},{7,5},{8,10},{9,11},{10,... | collective-permute-start | bytes 393224 | tf_op jit(solution)/shard_map/ppermute | solution.py:405
  123.0 14.1 %collective-permute-start.22 = (bf16[128,640]{1,0:T(8,128)(2,1)S(1)}, bf16[128,640]{1,0:T(8,128)(2,1)S(1)}, u32[]{:S(2)}, u32[]{:S(2)}) collective-permute-start(bf16[128,640]{1,0:T(8,128)(2,1)S(1)} %get-tuple-element.39), channel_id=1, source_target_pairs={{0,2},{1,3},{2,0},{3,1},{4,6},{5,7},{6,4},{7,5},{8,10},{9,11},{10,... | collective-permute-start | bytes 491528 | tf_op jit(solution)/shard_map/ppermute | solution.py:405
  123.2 14.0 %collective-permute-start.19 = (bf16[128,512]{1,0:T(8,128)(2,1)S(1)}, bf16[128,512]{1,0:T(8,128)(2,1)S(1)}, u32[]{:S(2)}, u32[]{:S(2)}) collective-permute-start(bf16[128,512]{1,0:T(8,128)(2,1)S(1)} %get-tuple-element.41), channel_id=1, source_target_pairs={{0,2},{1,3},{2,0},{3,1},{4,6},{5,7},{6,4},{7,5},{8,10},{9,11},{10,... | collective-permute-start | bytes 393224 | tf_op jit(solution)/shard_map/ppermute | solution.py:405
  139.8 3.6 %collective-permute-start.23 = (f32[8,128]{1,0:T(8,128)S(1)}, f32[8,128]{1,0:T(8,128)S(1)}, u32[]{:S(2)}, u32[]{:S(2)}) collective-permute-start(f32[8,128]{1,0:T(8,128)S(1)} %get-tuple-element.38), channel_id=1, source_target_pairs={{0,8},{4,12},{8,0},{12,4},{1,9},{5,13},{9,1},{13,5},{2,10},{6,14},... | collective-permute-start | bytes 12296 | tf_op jit(solution)/shard_map/ppermute | solution.py:419
  143.4 9.9 %collective-permute-start.24 = (f32[8,128]{1,0:T(8,128)S(1)}, f32[8,128]{1,0:T(8,128)S(1)}, u32[]{:S(2)}, u32[]{:S(2)}) collective-permute-start(f32[8,128]{1,0:T(8,128)S(1)} %add.38), channel_id=1, source_target_pairs={{0,4},{4,0},{8,12},{12,8},{1,5},{5,1},{9,13},{13,9},{2,6},{6,2},{1... | collective-permute-start | bytes 12296 | tf_op jit(solution)/shard_map/ppermute | solution.py:419
  (2 other events, 1.8 us)

commit v2 on v0

v2 whole, which is shorter than its diff:
```python
import functools
import math

import jax
import jax.numpy as jnp
from jax import lax
from jax.experimental import pallas as pl
from jax.experimental.pallas import tpu as pltpu
from jax.sharding import PartitionSpec as P

LANES = 128
NT = (((1,), (1,)), ((), ()))
TN = (((0,), (0,)), ((), ()))
VMEM_LIMIT = 24 * 1024 * 1024


def dot(a, b, dims, precision=None):
    return lax.dot_general(a, b, dims, precision=precision, preferred_element_type=jnp.float32)


def pairs(size, bit):
    return [(at, at ^ bit) for at in range(size)]


def bits_of(size):
    return [1 << at for at in reversed(range(size.bit_length() - 1))]


def params():
    return pltpu.CompilerParams(vmem_limit_bytes=VMEM_LIMIT)


def cost(flops, bytes_accessed):
    return pl.CostEstimate(flops=flops // 100, bytes_accessed=bytes_accessed // 100, transcendentals=0)


def project_kernel(order, tile, me, *refs):
    sources, (sent, kept, gram, gram_low), (held, whole, arrived) = refs[:10], refs[10:14], (refs[14:23], refs[23], refs[24])
    copies = {}

    def copy(name, source, target):
        one = pltpu.make_async_copy(source, target, arrived.at[len(copies)])
        one.start()
        copies[name] = one

    up_in, gate, up_pre, grad_h, grad_o, p_ui, p_uo, p_di, p_do, old = sources
    h_up_in, h_gate, h_up_pre, h_grad_h, h_grad_o, h_ui, h_uo, h_di, h_do = held
    starts = range(0, h_gate.shape[1], tile)
    for start in starts:
        part = pl.ds(start, tile)
        for name, source, target in (("gate", gate, h_gate), ("grad_h", grad_h, h_grad_h), ("up_pre", up_pre, h_up_pre)):
            copy((name, start), source.at[0, :, part], target.at[:, part])
        for name, source, target in (("uo", p_uo, h_uo), ("di", p_di, h_di)):
            copy((name, start), source.at[:, part], target.at[:, part])
    copy("up_in", up_in.at[0], h_up_in)
    copy("ui", p_ui, h_ui)
    copy("grad_o", grad_o.at[0], h_grad_o)
    copy("do", p_do, h_do)
    share = gram.shape[0] // 4
    for at in range(4):
        rows = pl.ds(at * share, share)
        copy(("gram", at), old.at[rows], gram.at[rows])

    out_up, in_down = 0.0, 0.0
    for start in starts:
        part = slice(start, start + tile)
        for name in ("gate", "grad_h", "up_pre", "uo", "di"):
            copies[name, start].wait()
        act = h_gate[:, part].astype(jnp.float32)
        act = act / (1.0 + jnp.exp(-act))
        grad_up = (h_grad_h[:, part].astype(jnp.float32) * act).astype(jnp.bfloat16)
        hidden = (act * h_up_pre[:, part].astype(jnp.float32)).astype(jnp.bfloat16)
        out_up = out_up + dot(grad_up, h_uo[:, part], NT)
        in_down = in_down + dot(hidden, h_di[:, part], NT)
    for name in ("up_in", "ui", "grad_o", "do"):
        copies[name].wait()
    in_up = dot(h_up_in[...], h_ui[...], NT)
    out_down = dot(h_grad_o[...], h_do[...], NT)
    whole[...] = jnp.concatenate([in_up, out_up, in_down, out_down], axis=1)
    rows = whole.shape[0] // len(order)
    own = me[0] % len(order)
    for at, code in enumerate(order):
        out = sent if at < len(order) // 2 else kept
        spot = at % (len(order) // 2) * rows
        out[spot : spot + rows, :] = whole[pl.ds(pl.multiple_of((own ^ code) * rows, rows), rows), :]
    for at in range(4):
        copies["gram", at].wait()
        rows = slice(at * share, (at + 1) * share)
        gram_low[rows, :] = gram[rows, :].astype(jnp.bfloat16)


def project_all(order, me, up_in, gate, up_pre, grad_h, grad_o, p_ui, p_uo, p_di, p_do, gram):
    _, seq, d_here = up_in.shape
    f_here = gate.shape[2]
    rank = p_ui.shape[0]
    tile = max(t for t in range(LANES, 897, LANES) if f_here % t == 0)
    arrays = (up_in, gate, up_pre, grad_h, grad_o, p_ui, p_uo, p_di, p_do)
    vmem = pl.BlockSpec(memory_space=pltpu.VMEM)
    return pl.pallas_call(
        functools.partial(project_kernel, order, tile),
        out_shape=[jax.ShapeDtypeStruct((seq // 2, 4 * rank), jnp.float32)] * 2
        + [jax.ShapeDtypeStruct(gram.shape, dtype) for dtype in (jnp.float32, jnp.bfloat16)],
        in_specs=[pl.BlockSpec(memory_space=pltpu.SMEM)] + [pl.BlockSpec(memory_space=pltpu.HBM)] * 10,
        out_specs=[vmem] * 4,
        scratch_shapes=[pltpu.VMEM(array.shape[-2:], array.dtype) for array in arrays]
        + [
            pltpu.VMEM((seq, 4 * rank), jnp.float32),
            pltpu.SemaphoreType.DMA((5 * (f_here // tile) + 8,)),
        ],
        compiler_params=params(),
        cost_estimate=cost(4 * seq * rank * (d_here + f_here), 6 * seq * f_here + 4 * seq * d_here),
    )(me, *(pltpu.with_memory_space_constraint(array, pltpu.HBM) for array in (*arrays, gram)))


def feature_kernel(norm, rank, mine, there, out, square):
    rows = there.shape[0]
    total = mine[mine.shape[0] - rows :, :] + there[...]
    half = rank * rank // LANES
    for at in range(2):
        left = total[:, (2 * at + 1) * rank : (2 * at + 2) * rank]
        right = total[:, 2 * at * rank : (2 * at + 1) * rank]
        square[...] = dot(left, right, TN, lax.Precision.HIGHEST) * norm
        step = LANES // rank
        out[at * half : (at + 1) * half, :] = jnp.concatenate(
            [square[pl.ds(lane, half, step), :] for lane in range(step)], axis=1
        )


def feature_rows(norm, rank, mine, there):
    return pl.pallas_call(
        functools.partial(feature_kernel, norm, rank),
        out_shape=jax.ShapeDtypeStruct((2 * rank * rank // LANES, LANES), jnp.float32),
        scratch_shapes=[pltpu.VMEM((rank, rank), jnp.float32)],
        compiler_params=params(),
        cost_estimate=cost(24 * rank * rank * there.shape[0], 100000),
    )(mine, there)


def spread_kernel(seqs, dp, mp, me, gathered, left, right, col, rows_f, cols_f):
    grp_at, dp_at, mp_at = me[0] // (dp * mp), (me[0] // mp) % dp, me[0] % mp
    own = grp_at * dp + dp_at
    row_at = grp_at * mp + mp_at
    count = seqs.bit_length() - 1
    row_groups, col_groups = rows_f.shape[1] // LANES, cols_f.shape[1] // LANES
    for seq in range(seqs):
        code = own ^ seq
        place = 0
        for bit in range(count):
            place = place + (((code >> bit) & 1) << (count - 1 - bit))
        for group in range(row_groups):
            rows_f[seq : seq + 1, group * LANES : (group + 1) * LANES] = gathered[
                place, pl.ds(row_at * row_groups + group, 1), :
            ]
        for group in range(col_groups):
            cols_f[seq : seq + 1, group * LANES : (group + 1) * LANES] = gathered[
                place, pl.ds(dp_at * col_groups + group, 1), :
            ]
    row, column = rows_f[...], cols_f[...]
    row_high = row.astype(jnp.bfloat16).astype(jnp.float32)
    col_high = column.astype(jnp.bfloat16).astype(jnp.float32)
    row_low, col_low = row - row_high, column - col_high
    for out, stack in (
        (left, [row_high, row_high, row_low]),
        (right, [col_high, col_low, col_high]),
    ):
        spare = out.shape[0] - len(stack) * seqs
        if spare:
            stack.append(jnp.zeros((spare, out.shape[1]), jnp.float32))
        out[...] = jnp.concatenate(stack).astype(jnp.bfloat16)
    col[...] = column


def spread(me, gathered, dp, mp, rows_here, cols_here):
    seqs = gathered.shape[0]
    deep = -(-3 * seqs // 16) * 16
    return pl.pallas_call(
        functools.partial(spread_kernel, seqs, dp, mp),
        out_shape=[
            jax.ShapeDtypeStruct((deep, rows_here), jnp.bfloat16),
            jax.ShapeDtypeStruct((deep, cols_here), jnp.bfloat16),
            jax.ShapeDtypeStruct((seqs, cols_here), jnp.float32),
        ],
        in_specs=[
            pl.BlockSpec(memory_space=pltpu.SMEM),
            pl.BlockSpec(memory_space=pltpu.VMEM),
        ],
        scratch_shapes=[
            pltpu.VMEM((seqs, rows_here), jnp.float32),
            pltpu.VMEM((seqs, cols_here), jnp.float32),
        ],
        compiler_params=params(),
        cost_estimate=cost(0, 1000000),
    )(me, gathered)


def update_kernel(scale, me, gram, left, right, out):
    rows = out.shape[0]
    at = pl.ds(pl.multiple_of(pl.program_id(0) * rows, rows), rows)
    out[...] = gram[at, :] + dot(left[...], right[...], TN) * scale


def update(scale, me, gram, left, right):
    rows, cols = gram.shape
    tile = min(rows, 256)
    deep = left.shape[0]
    return pl.pallas_call(
        functools.partial(update_kernel, scale),
        out_shape=jax.ShapeDtypeStruct(gram.shape, jnp.float32),
        grid=(rows // tile,),
        in_specs=[
            pl.BlockSpec(memory_space=pltpu.SMEM),
            pl.BlockSpec(memory_space=pltpu.VMEM),
            pl.BlockSpec((deep, tile), lambda i: (0, i)),
            pl.BlockSpec((deep, cols), lambda i: (0, 0)),
        ],
        out_specs=pl.BlockSpec((tile, cols), lambda i: (i, 0)),
        compiler_params=params(),
        cost_estimate=cost(2 * rows * cols * deep, 8 * rows * cols),
    )(me, gram, left, right)


def place(me, sizes, direct, bits, at, row, per):
    grp, dp, mp = sizes
    target = ((at ^ ((me // mp) % dp)) * per + row) if direct else row
    code = target ^ ((me // (dp * mp)) * mp + me % mp)
    spot = 0
    for bit in bits:
        spot = 2 * spot + (1 - ((code // bit) & 1))
    return spot


def sort_rows(me, sizes, direct, bits, first, count, cans, out):
    for at, can in enumerate(cans):
        for row in range(can.shape[0]):
            spot = place(me, sizes, direct, bits, at, row, can.shape[0]) - first

            @pl.when((spot >= 0) & (spot < count))
            def _(can=can, row=row, spot=spot):
                out[spot] = can[row]


def product_kernel(sizes, direct, bits, first, start, n_cans, n_recv, me, *refs):
    cans, gram, recvs, outs = refs[:n_cans], refs[n_cans], refs[n_cans + 1 : n_cans + 1 + n_recv], refs[n_cans + 1 + n_recv :]
    outs, rows = outs[:-1], outs[-1]
    low = outs[0]
    count, unit, depth = rows.shape
    sort_rows(me[0], sizes, direct, bits, first, count, cans, rows)
    width = low.shape[1]
    tile = min(width, 512)
    for at in range(0, width, tile):
        value = dot(
            rows[...].reshape(count * unit, depth),
            gram[:, start + at : start + at + tile],
            (((1,), (0,)), ((), ())),
        )
        if not recvs:
            low[:, at : at + tile] = value.astype(jnp.bfloat16)
        else:
            value = value + recvs[0][:, at : at + tile].astype(jnp.float32)
            half = low.shape[0]
            low[:, at : at + tile] = value[:half].astype(jnp.bfloat16)
            outs[1][:, at : at + tile] = value[half:]


def product(sizes, direct, bits, me, cans, gram, recvs, start, width):
    depth = gram.shape[0]
    unit = cans[0].shape[1]
    count = sizes[0] * sizes[2] // 2
    rows = count * unit
    vmem = pl.BlockSpec(memory_space=pltpu.VMEM)
    args = [me, *cans, gram, *recvs]
    if recvs:
        out_shape = [
            jax.ShapeDtypeStruct((rows // 2, width), jnp.bfloat16),
            jax.ShapeDtypeStruct((rows // 2, width), jnp.float32),
        ]
    else:
        out_shape = [jax.ShapeDtypeStruct((rows, width), jnp.bfloat16)]
    first = count if recvs else 0
    return pl.pallas_call(
        functools.partial(product_kernel, sizes, direct, bits, first, start, len(cans), len(recvs)),
        out_shape=out_shape,
        in_specs=[pl.BlockSpec(memory_space=pltpu.SMEM)] + [vmem] * (len(args) - 1),
        out_specs=[vmem] * len(out_shape),
        scratch_shapes=[pltpu.VMEM((count, unit, depth), jnp.bfloat16)],
        compiler_params=params(),
        cost_estimate=cost(2 * rows * width * depth, 2 * depth * width + 2 * rows * (depth + width)),
    )(*args)


def thin_kernel(sizes, direct, bits, n_cans, seqs, me, *refs):
    halves = refs[:n_cans], refs[n_cans : 2 * n_cans]
    gram, row, col, out, rows = refs[2 * n_cans :]
    count, _, unit, depth = rows.shape
    for half, cans in enumerate(halves):
        for at, can in enumerate(cans):
            for spot in range(can.shape[0]):
                rows[place(me[0], sizes, direct, bits, at, spot, can.shape[0]), half] = can[spot]

    def stack(*values):
        split = []
        for value in values:
            high = value.astype(jnp.bfloat16).astype(jnp.float32)
            split += [high, value - high]
        spare = -len(split) * seqs % LANES
        if spare:
            split.append(jnp.zeros((spare, values[0].shape[1]), jnp.float32))
        return jnp.concatenate(split).astype(jnp.bfloat16)

    across = dot(gram[...], stack(col[...]), NT).T
    across = across[:seqs] + across[seqs : 2 * seqs]
    own = row[:seqs].astype(jnp.float32) + row[2 * seqs : 3 * seqs].astype(jnp.float32)
    value = dot(rows[...].reshape(-1, depth), stack(own, across), NT).T
    out[:seqs] = value[:seqs] + value[seqs : 2 * seqs]
    out[seqs:] = value[2 * seqs : 3 * seqs] + value[3 * seqs : 4 * seqs]


def thin_products(sizes, direct, bits, me, halves, gram, left, col):
    seqs = col.shape[0]
    count = sizes[0] * sizes[2]
    unit, depth = halves[0][0].shape[1:]
    rows = count * 2 * unit
    vmem = pl.BlockSpec(memory_space=pltpu.VMEM)
    args = [*halves[0], *halves[1], gram, left, col]
    return pl.pallas_call(
        functools.partial(thin_kernel, sizes, direct, bits, len(halves[0]), seqs),
        out_shape=jax.ShapeDtypeStruct((2 * seqs, rows), jnp.float32),
        in_specs=[pl.BlockSpec(memory_space=pltpu.SMEM)] + [vmem] * len(args),
        out_specs=vmem,
        scratch_shapes=[pltpu.VMEM((count, 2, unit, depth), jnp.bfloat16)],
        compiler_params=params(),
        cost_estimate=cost(256 * depth * (gram.shape[1] + rows), 2 * depth * (gram.shape[1] + rows)),
    )(me, *args)


def score_kernel(scale, norm, thin, col, out):
    column = col[...]
    seqs = column.shape[0]
    inner = dot(column, column, NT, lax.Precision.HIGHEST) * scale
    value = thin[seqs:] + dot(inner, thin[:seqs], (((1,), (0,)), ((), ())), lax.Precision.HIGHEST)
    out[...] = value * norm


def score(scale, norm, thin, col):
    return pl.pallas_call(
        functools.partial(score_kernel, scale, norm),
        out_shape=jax.ShapeDtypeStruct((col.shape[0], thin.shape[1]), jnp.float32),
        compiler_params=params(),
        cost_estimate=cost(12 * col.size * col.shape[0], 8 * col.size),
    )(thin, col)


def finish_kernel(seqs, scale, norm, spots, *refs):
    terms, (thin, col, mapped) = list(refs[:-3]), refs[-3:]
    for number, row, column, rows, width in spots:
        value = 0.0
        for _ in range(number):
            term = terms.pop(0)
            value = value + term[term.shape[0] - rows :, :].astype(jnp.float32)
        share = dot(thin[:seqs, row : row + rows], col[:, column : column + width], TN, lax.Precision.HIGHEST)
        mapped[row : row + rows, column : column + width] = ((value + share * scale) * norm).astype(jnp.bfloat16)


def finish(scale, norm, kept, thin, col, chunk):
    seqs, cols = col.shape
    spots, args = [], []
    for terms, row, column, rows, width in kept:
        spots.append((len(terms), row, column, rows, width))
        args += terms
    return pl.pallas_call(
        functools.partial(finish_kernel, seqs, scale, norm, spots),
        out_shape=jax.ShapeDtypeStruct((chunk, cols), jnp.bfloat16),
        compiler_params=params(),
        cost_estimate=cost(12 * chunk * cols * seqs, 12 * chunk * cols),
    )(*args, thin, col)


def after(value, *others):
    return lax.optimization_barrier((value, *others))[0]


def shards(
    sizes,
    up_input,
    gate_pre,
    up_pre,
    grad_hidden,
    grad_output,
    proj_up_in,
    proj_up_out,
    proj_down_in,
    proj_down_out,
    gram,
    canaries,
):
    grp, dp, mp = sizes
    rank = proj_up_in.shape[0]
    seq_len = up_input.shape[1]
    rows_here, cols_here = gram.shape
    features = rows_here * grp * mp
    can_here, depth = canaries.shape
    chunk = can_here * dp // (grp * mp)
    seqs = grp * dp
    scale, norm = 1.0 / seqs, 1.0 / math.sqrt(features)
    me = lax.axis_index(("grp", "dp", "mp")).astype(jnp.int32).reshape(1)

    steps_grp = [("grp", grp, bit, bit * mp) for bit in bits_of(grp)]
    steps_mp = [("mp", mp, bit, bit) for bit in reversed(bits_of(mp))]
    grp_first, mp_first = steps_grp + steps_mp, steps_mp + steps_grp

    direct = can_here >= chunk
    half_rows = chunk // 2

    def spread_canaries(own, gate):
        blocks = {0: own}
        for bit in bits_of(dp):
            there = {at ^ bit: lax.ppermute(block, "dp", pairs(dp, bit)) for at, block in blocks.items()}
            blocks |= {at: after(block, gate) if bit > 1 else block for at, block in there.items()}
        return [blocks[at] for at in range(dp)]

    def begin(half, steps, start, width, gate):
        bits = [code for _, _, _, code in steps]
        (low,) = product(sizes, direct, bits, after(me, gate), halves[half], gram_low, [], start, width)
        return low

    def send(steps, low):
        axis, size, bit, _ = steps[0]
        return lax.ppermute(low, axis, pairs(size, bit))

    def add_first(half, steps, start, width, recv, gate):
        bits = [code for _, _, _, code in steps]
        low, keep = product(
            sizes, direct, bits, after(me, gate), halves[half], gram_low, [recv], start, width
        )
        axis, size, bit, _ = steps[1]
        return keep, [lax.ppermute(low, axis, pairs(size, bit))]

    def add_next(steps, keep, arrived, gate):
        left_over = 1 << (len(steps) - 1 - len(arrived))
        rows = (left_over // 2) * half_rows
        low = keep[:rows]
        for array in arrived:
            low = low + array[-left_over * half_rows :][:rows].astype(jnp.float32)
        low = after(low.astype(jnp.bfloat16), gate)
        axis, size, bit, _ = steps[len(arrived) + 1]
        return low, keep[rows:], [*arrived, lax.ppermute(low, axis, pairs(size, bit))]

    if direct:
        own = canaries.reshape(-1, 2, half_rows, depth)
    else:
        own = lax.all_gather(canaries, "dp", axis=0, tiled=True).reshape(-1, 2, half_rows, depth)

    order = [0]
    for _, _, _, code in reversed(steps_mp):
        order = [at | code for at in order] + order
    sent, token_sums, gram_here, gram_low = project_all(
        order, me, up_input, gate_pre, up_pre, grad_hidden, grad_output,
        proj_up_in, proj_up_out, proj_down_in, proj_down_out, gram,
    )
    halves = [spread_canaries(own[:, 0], gram_low) if direct else [own[:, 0]]]
    middle = cols_here // 2
    low_a = begin(0, grp_first, 0, middle, gram_low)
    recv_a = send(grp_first, low_a)
    gate = low_a
    for axis, size, bit, _ in steps_mp[:-1]:
        token_sums = token_sums[-sent.shape[0] :] + after(lax.ppermute(sent, axis, pairs(size, bit)), gate)
        sent = token_sums[: token_sums.shape[0] // 2]
    there = lax.ppermute(sent, "mp", pairs(mp, steps_mp[-1][2]))
    halves.append(spread_canaries(own[:, 1], token_sums) if direct else [own[:, 1]])
    low_c = begin(1, mp_first, middle, middle, token_sums)
    recv_c = send(mp_first, low_c)
    row = feature_rows(1.0 / math.sqrt(seq_len), rank, token_sums, after(there, low_c))[None]

    gathered = row
    low_d = begin(0, grp_first, middle, middle, row)
    recv_d = send(grp_first, low_d)
    keep_a, there_a = add_first(0, grp_first, 0, middle, recv_a, low_d)
    gate = keep_a
    for bit in bits_of(grp):
        gathered = jnp.concatenate([gathered, after(lax.ppermute(gathered, "grp", pairs(grp, bit)), gate)])
    low_b = begin(1, grp_first, 0, middle, gathered)
    gate = low_b
    for at, bit in enumerate(reversed(bits_of(mp))):
        gathered = gathered + after(lax.ppermute(gathered, "mp", pairs(mp, bit)), gate)
        if at == 0:
            keep_c, there_c = add_first(1, mp_first, middle, middle, recv_c, gathered)
            gate = keep_c
    recv_b = send(grp_first, after(low_b, gathered))
    keep_d, there_d = add_first(0, grp_first, middle, middle, recv_d, gathered)
    gate = keep_d
    for bit in bits_of(dp):
        gathered = jnp.concatenate([gathered, after(lax.ppermute(gathered, "dp", pairs(dp, bit)), gate)])
        if bit == bits_of(dp)[0]:
            low_a, keep_a, there_a = add_next(grp_first, keep_a, there_a, gathered)
            gate = low_a
    left, right, col = spread(me, gathered, dp, mp, rows_here, cols_here)
    thin = thin_products(
        sizes, direct, [code for _, _, _, code in grp_first], me, halves, gram_low, left, col
    )
    gram_new = update(scale, after(me, thin), gram_here, left, right)
    keep_b, there_b = add_first(1, grp_first, 0, middle, recv_b, gram_new)
    low_c, keep_c, there_c = add_next(mp_first, keep_c, there_c, keep_b)
    low_d, keep_d, there_d = add_next(grp_first, keep_d, there_d, low_c)
    gate = low_d
    for at, (axis, size, bit, _) in enumerate(grp_first):
        half = thin.shape[1] // 2
        thin = thin[:, half:] + after(lax.ppermute(thin[:, :half], axis, pairs(size, bit)), gate)
        if at == 0:
            low_b, keep_b, there_b = add_next(grp_first, keep_b, there_b, thin)
            gate = low_b
    scores = score(scale, norm * norm, thin, col)
    for bit in bits_of(dp):
        scores = scores + lax.ppermute(scores, "dp", pairs(dp, bit))
    kept = [
        ([keep_a, *there_a], 0, 0, half_rows, middle),
        ([keep_d, *there_d], 0, middle, half_rows, middle),
        ([keep_c, *there_c], half_rows, middle, half_rows, middle),
        ([keep_b, *there_b], half_rows, 0, half_rows, middle),
    ]
    mapped = finish(scale, norm, kept, thin, col, chunk)
    return gram_new, mapped, scores


def solution(mesh):
    sizes = tuple(mesh.shape[name] for name in ("grp", "dp", "mp"))
    wide = P(("grp", "dp"), None, "mp")
    return jax.shard_map(
        functools.partial(shards, sizes),
        mesh=mesh,
        in_specs=(wide, wide, wide, wide, wide)
        + (P(None, "mp"),) * 4
        + (P(("grp", "mp"), "dp"), P("dp", ("grp", "mp"))),
        out_specs=(P(("grp", "mp"), "dp"), P(("grp", "mp"), "dp"), P(None, ("grp", "mp"))),
        check_vma=False,
    )
```

time: 263 us -> 92.9 us (0.35)
  waiting for transfers between devices: 190 us -> 30 us
  starting transfers between devices: 0.12 us -> 37 us
  matrix products: 36.5 us -> 0 us
  Pallas kernels: 0 us -> 22.9 us
  blocking collectives: 16.8 us -> 0 us
  between operations: 15.6 us -> 0.85 us
    reduce_scatter x1 -> x0, waiting for transfers between devices: 148 us -> none  [shards(): lax.psum_scatter(jnp.dot(gathered, gram_low, preferred_element_type=jnp.f...]
    psum x1 -> x0, waiting for transfers between devices: 41.2 us -> none  [shards(): lax.psum((project(up_input[0], proj_up_in), project(grad_up, proj_up_out)...]
    ppermute x0 -> x30, starting transfers between devices: none -> 37 us  [the longest x4 6.95 us: add_first(): return (keep, [lax.ppermute(low, axis, pairs(size, bit))])]
    dot_general x9 -> x0, matrix products: 36.5 us -> none  [the longest x1 11.8 us: shards(): jnp.dot(gathered, gram_low, preferred_element_type=jnp.float32)]
    ppermute x0 -> x30, waiting for transfers between devices: none -> 30 us  [the longest x2 6.61 us: shards(): lax.ppermute(gathered, 'mp', pairs(mp, bit))]
    pallas_call x0 -> x15, Pallas kernels: none -> 22.9 us  [the longest x8 6.87 us: product(): pl.pallas_call(functools.partial(product_kernel, sizes, direct, bits, fir...]
    all_gather x1 -> x0, blocking collectives: 9.33 us -> none  [shards(): feature_rows = lax.all_gather(own_row, ('grp', 'dp'), axis=0, tiled=True)]
    psum x1 -> x0, blocking collectives: 7.42 us -> none  [shards(): lax.psum(jnp.dot(right_block, mapped_share.T, precision=lax.Precision.HIG...]
  transfers between devices with their start and end apart: 3 -> 30, of which waited for: 2 -> 14; matrix products, arithmetic and copies ran while one was open for 5% -> 1% of each run, Pallas kernels for 0% -> 23%
where the time goes in v2:
time: 92.9 us; the launch traced here: 92.7 us
  starting transfers between devices  37 us (40%)
  waiting for transfers between devices  30 us (32%)
  Pallas kernels  22.9 us (25%)
  local copies, waits for them, and re-layouts  1.09 us (1%)
    ppermute x4, starting transfers between devices, add_first(): return (keep, [lax.ppermute(low, axis, pairs(size, bit))])  6.95 us
    pallas_call x8, Pallas kernels, product(): pl.pallas_call(functools.partial(product_kernel, sizes, direct, bits, fir...  6.87 us
    ppermute x2, waiting for transfers between devices, shards(): lax.ppermute(gathered, 'mp', pairs(mp, bit))  6.61 us
    ppermute x4, starting transfers between devices, add_next(): lax.ppermute(low, axis, pairs(size, bit))  6.19 us
    pallas_call x1, Pallas kernels, project_all(): pl.pallas_call(functools.partial(project_kernel, order, tile), out_shape=...  6.08 us
    ppermute x4, starting transfers between devices, send(): return lax.ppermute(low, axis, pairs(size, bit))  5 us
    ppermute x6, starting transfers between devices, spread_canaries(): lax.ppermute(block, 'dp', pairs(dp, bit))  4.85 us
    ppermute x4, waiting for transfers between devices, add_first(): return (keep, [lax.ppermute(low, axis, pairs(size, bit))])  4.5 us
  transfers between devices with their start and end apart: 30, of which 14 were waited for; matrix products, arithmetic and copies ran while one was open for 1% of the time, Pallas kernels for 23%

profile of v2, /device:TPU:0, one launch (start us, length us, event | category | flops | bytes accessed | tf_op | source)
XLA Modules:
  0.0 92.7 jit_solution(8126370147965096893)
XLA Ops:
  0.6 1.1 %slice_bitcast_fusion = (bf16[2,64,1024]{2,1,0:T(8,128)(2,1)S(1)}, bf16[2,64,1024]{2,1,0:T(8,128)(2,1)S(1)}) fusion(bf16[2,2,64,1024]{3,2,1,0:T(8,128)(2,1)} %bitcast.15), kind=kLoop, calls=%fused_computation | loop fusion | bytes 1048576 | tf_op jit(solution)/shard_map/squeeze | solution.py:469
  1.7 3.0 %collective-permute-start.1 = (bf16[2,64,1024]{2,1,0:T(8,128)(2,1)S(1)}, bf16[2,64,1024]{2,1,0:T(8,128)(2,1)S(1)}, u32[]{:S(2)}, u32[]{:S(2)}) collective-permute-start(bf16[2,64,1024]{2,1,0:T(8,128)(2,1)S(1)} %get-tuple-element.94.refs_0_), channel_id=1, source_target_pairs={{0,8},{4,12},{8,0},{12,4},{1,9},{5,13},{9,1},{13,5},{2,10},{6,14},... | collective-permute-start | bytes 786440 | tf_op jit(solution)/shard_map/ppermute | solution.py:417
  4.7 6.1 %shard_map.130 = (f32[128,256]{1,0:T(8,128)S(1)}, f32[128,256]{1,0:T(8,128)S(1)}, f32[1024,2048]{1,0:T(8,128)S(1)}, bf16[1024,2048]{1,0:T(8,128)(2,1)S(1)}) custom-call(s32[1]{0:T(128)} %bitcast.me, bf16[1,256,1024]{2,1,0:T(8,128)(2,1)} %refs_0_.1, bf16[1,256,3584]{2,1,0:T(8,128)(2,1)} %refs_1_.1, bf16[1,256,3584]{2,1,0:T(8,128)(2,1)} %refs_2_.1, ...), custom_call_target="tpu_custom_call" | custom-call | flops 3019898 | bytes 65536 | tf_op jit(solution)/shard_map/pallas_call | solution.py:99
  11.4 1.4 %collective-permute-start.4 = (bf16[2,64,1024]{2,1,0:T(8,128)(2,1)S(1)}, bf16[2,64,1024]{2,1,0:T(8,128)(2,1)S(1)}, u32[]{:S(2)}, u32[]{:S(2)}) collective-permute-start(bf16[2,64,1024]{2,1,0:T(8,128)(2,1)S(1)} %get-tuple-element.93.refs_0_.refs_4_), channel_id=1, source_target_pairs={{0,8},{4,12},{8,0},{12,4},{1,9},{5,13},{9,1},{13,5},{2,10},{6,14},... | collective-permute-start | bytes 786440 | tf_op jit(solution)/shard_map/ppermute | solution.py:417
  13.6 1.6 %collective-permute-start.9 = (bf16[256,1024]{1,0:T(8,128)(2,1)S(1)}, bf16[256,1024]{1,0:T(8,128)(2,1)S(1)}, u32[]{:S(2)}, u32[]{:S(2)}) collective-permute-start(bf16[256,1024]{1,0:T(8,128)(2,1)S(1)} %shard_map.131), channel_id=1, source_target_pairs={{0,16},{16,0},{1,17},{17,1},{2,18},{18,2},{3,19},{19,3},{4,20},{20... | collective-permute-start | bytes 1572872 | tf_op jit(solution)/shard_map/ppermute | solution.py:428
  15.2 1.6 %collective-permute-start.5 = (f32[128,256]{1,0:T(8,128)S(1)}, f32[128,256]{1,0:T(8,128)S(1)}, u32[]{:S(2)}, u32[]{:S(2)}) collective-permute-start(f32[128,256]{1,0:T(8,128)S(1)} %get-tuple-element.47), channel_id=1, source_target_pairs={{0,1},{1,0},{2,3},{3,2},{4,5},{5,4},{6,7},{7,6},{8,9},{9,8},{10,11... | collective-permute-start | bytes 393224 | tf_op jit(solution)/shard_map/ppermute | solution.py:466
  16.8 3.8 %collective-permute-done.5 = f32[128,256]{1,0:T(8,128)S(1)} collective-permute-done((f32[128,256]{1,0:T(8,128)S(1)}, f32[128,256]{1,0:T(8,128)S(1)}, u32[]{:S(2)}, u32[]{:S(2)}) %collective-permute-start.5) | collective-permute-done | bytes 131104 | tf_op jit(solution)/shard_map/ppermute | solution.py:466
  20.7 2.7 %collective-permute-start.7 = (f32[64,256]{1,0:T(8,128)S(1)}, f32[64,256]{1,0:T(8,128)S(1)}, u32[]{:S(2)}, u32[]{:S(2)}) collective-permute-start(f32[64,256]{1,0:T(8,128)S(1)} %slice.86), channel_id=1, source_target_pairs={{0,2},{1,3},{2,0},{3,1},{4,6},{5,7},{6,4},{7,5},{8,10},{9,11},{10,... | collective-permute-start | bytes 196616 | tf_op jit(solution)/shard_map/ppermute | solution.py:468
  24.2 1.7 %collective-permute-start.12 = (bf16[256,1024]{1,0:T(8,128)(2,1)S(1)}, bf16[256,1024]{1,0:T(8,128)(2,1)S(1)}, u32[]{:S(2)}, u32[]{:S(2)}) collective-permute-start(bf16[256,1024]{1,0:T(8,128)(2,1)S(1)} %shard_map.132), channel_id=1, source_target_pairs={{0,1},{1,0},{2,3},{3,2},{4,5},{5,4},{6,7},{7,6},{8,9},{9,8},{10,11... | collective-permute-start | bytes 1572872 | tf_op jit(solution)/shard_map/ppermute | solution.py:428
  25.9 1.7 %collective-permute-done.7.there = f32[64,256]{1,0:T(8,128)S(1)} collective-permute-done((f32[64,256]{1,0:T(8,128)S(1)}, f32[64,256]{1,0:T(8,128)S(1)}, u32[]{:S(2)}, u32[]{:S(2)}) %collective-permute-start.7) | collective-permute-done | bytes 65568 | tf_op jit(solution)/shard_map/ppermute | solution.py:468
  30.6 1.4 %collective-permute-done.8 = f32[1,64,128]{2,1,0:T(8,128)S(1)} collective-permute-done((f32[1,64,128]{2,1,0:T(8,128)S(1)}, f32[1,64,128]{2,1,0:T(8,128)S(1)}, u32[]{:S(2)}, u32[]{:S(2)}) %collective-permute-start.8) | collective-permute-done | bytes 32800 | tf_op jit(solution)/shard_map/ppermute | solution.py:480
  34.2 5.7 %collective-permute-done.10 = f32[2,64,128]{2,1,0:T(8,128)S(1)} collective-permute-done((f32[2,64,128]{2,1,0:T(8,128)S(1)}, f32[2,64,128]{2,1,0:T(8,128)S(1)}, u32[]{:S(2)}, u32[]{:S(2)}) %collective-permute-start.10) | collective-permute-done | bytes 65568 | tf_op jit(solution)/shard_map/ppermute | solution.py:484
  40.0 1.6 %collective-permute-start.11 = (f32[2,64,128]{2,1,0:T(8,128)S(1)}, f32[2,64,128]{2,1,0:T(8,128)S(1)}, u32[]{:S(2)}, u32[]{:S(2)}) collective-permute-start(f32[2,64,128]{2,1,0:T(8,128)S(1)} %fusion), channel_id=1, source_target_pairs={{0,2},{1,3},{2,0},{3,1},{4,6},{5,7},{6,4},{7,5},{8,10},{9,11},{10,... | collective-permute-start | bytes 196616 | tf_op jit(solution)/shard_map/ppermute | solution.py:484
  41.6 2.5 %collective-permute-start.16 = (bf16[128,1024]{1,0:T(8,128)(2,1)S(1)}, bf16[128,1024]{1,0:T(8,128)(2,1)S(1)}, u32[]{:S(2)}, u32[]{:S(2)}) collective-permute-start(bf16[128,1024]{1,0:T(8,128)(2,1)S(1)} %get-tuple-element.65), channel_id=1, source_target_pairs={{0,1},{1,0},{2,3},{3,2},{4,5},{5,4},{6,7},{7,6},{8,9},{9,8},{10,11... | collective-permute-start | bytes 786440 | tf_op jit(solution)/shard_map/ppermute | solution.py:436
  45.8 1.5 %collective-permute-start.13 = (f32[2,64,128]{2,1,0:T(8,128)S(1)}, f32[2,64,128]{2,1,0:T(8,128)S(1)}, u32[]{:S(2)}, u32[]{:S(2)}) collective-permute-start(f32[2,64,128]{2,1,0:T(8,128)S(1)} %fusion.3), channel_id=1, source_target_pairs={{0,8},{4,12},{8,0},{12,4},{1,9},{5,13},{9,1},{13,5},{2,10},{6,14},... | collective-permute-start | bytes 196616 | tf_op jit(solution)/shard_map/ppermute | solution.py:492
  48.3 1.4 %collective-permute-start.18 = (bf16[128,1024]{1,0:T(8,128)(2,1)S(1)}, bf16[128,1024]{1,0:T(8,128)(2,1)S(1)}, u32[]{:S(2)}, u32[]{:S(2)}) collective-permute-start(bf16[128,1024]{1,0:T(8,128)(2,1)S(1)} %get-tuple-element.73), channel_id=1, source_target_pairs={{0,1},{1,0},{2,3},{3,2},{4,5},{5,4},{6,7},{7,6},{8,9},{9,8},{10,11... | collective-permute-start | bytes 786440 | tf_op jit(solution)/shard_map/ppermute | solution.py:436
  49.8 2.4 %collective-permute-start.19 = (bf16[128,1024]{1,0:T(8,128)(2,1)S(1)}, bf16[128,1024]{1,0:T(8,128)(2,1)S(1)}, u32[]{:S(2)}, u32[]{:S(2)}) collective-permute-start(bf16[128,1024]{1,0:T(8,128)(2,1)S(1)} %get-tuple-element.74), channel_id=1, source_target_pairs={{0,2},{1,3},{2,0},{3,1},{4,6},{5,7},{6,4},{7,5},{8,10},{9,11},{10,... | collective-permute-start | bytes 786440 | tf_op jit(solution)/shard_map/ppermute | solution.py:436
  53.2 1.3 %collective-permute-done.15 = f32[4,64,128]{2,1,0:T(8,128)S(1)} collective-permute-done((f32[4,64,128]{2,1,0:T(8,128)S(1)}, f32[4,64,128]{2,1,0:T(8,128)S(1)}, u32[]{:S(2)}, u32[]{:S(2)}) %collective-permute-start.15) | collective-permute-done | bytes 131104 | tf_op jit(solution)/shard_map/ppermute | solution.py:492
  54.6 2.9 %shard_map.140 = f32[16,1024]{1,0:T(8,128)S(1)} custom-call(s32[1]{0:T(128)} %bitcast.me, bf16[2,64,1024]{2,1,0:T(8,128)(2,1)S(1)} %get-tuple-element.94.refs_0_, bf16[2,64,1024]{2,1,0:T(8,128)(2,1)S(1)} %collective-permute-done.refs_1_, bf16[2,64,1024]{2,1,0:T(8,128)(2,1)S(1)} %collective-permute-done.1.refs_2_, ...), custom_call_target="tpu_custom_call" | custom-call | flops 8053063 | bytes 62914 | tf_op jit(solution)/shard_map/pallas_call | solution.py:325
  57.5 4.3 %shard_map.141 = f32[1024,2048]{1,0:T(8,128)} custom-call(s32[1]{0:T(128)} %bitcast.me, f32[1024,2048]{1,0:T(8,128)S(1)} %get-tuple-element.71.gram, bf16[32,1024]{1,0:T(8,128)(2,1)S(1)} %get-tuple-element.68.refs_9_.left, bf16[32,2048]{1,0:T(8,128)(2,1)S(1)} %get-tuple-element.72.right), custom_call_target="tpu_custom_call" | custom-call | flops 1342177 | bytes 167772 | tf_op jit(solution)/shard_map/pallas_call | solution.py:206
  61.8 1.1 %collective-permute-start.24 = (f32[16,512]{1,0:T(8,128)S(1)}, f32[16,512]{1,0:T(8,128)S(1)}, u32[]{:S(2)}, u32[]{:S(2)}) collective-permute-start(f32[16,512]{1,0:T(8,128)S(1)} %slice.92), channel_id=1, source_target_pairs={{0,16},{16,0},{1,17},{17,1},{2,18},{18,2},{3,19},{19,3},{4,20},{20... | collective-permute-start | bytes 98312 | tf_op jit(solution)/shard_map/ppermute | solution.py:507
  63.0 1.6 %collective-permute-done.20.refs_5_ = bf16[256,1024]{1,0:T(8,128)(2,1)S(1)} collective-permute-done((bf16[256,1024]{1,0:T(8,128)(2,1)S(1)}, bf16[256,1024]{1,0:T(8,128)(2,1)S(1)}, u32[]{:S(2)}, u32[]{:S(2)}) %collective-permute-start.20) | collective-permute-done | bytes 524320 | tf_op jit(solution)/shard_map/ppermute | solution.py:428
  66.3 1.5 %collective-permute-start.26 = (f32[16,256]{1,0:T(8,128)S(1)}, f32[16,256]{1,0:T(8,128)S(1)}, u32[]{:S(2)}, u32[]{:S(2)}) collective-permute-start(f32[16,256]{1,0:T(8,128)S(1)} %slice.94), channel_id=1, source_target_pairs={{0,1},{1,0},{2,3},{3,2},{4,5},{5,4},{6,7},{7,6},{8,9},{9,8},{10,11... | collective-permute-start | bytes 49160 | tf_op jit(solution)/shard_map/ppermute | solution.py:507
  67.7 4.5 %collective-permute-done.23.refs_10_ = bf16[128,1024]{1,0:T(8,128)(2,1)S(1)} collective-permute-done((bf16[128,1024]{1,0:T(8,128)(2,1)S(1)}, bf16[128,1024]{1,0:T(8,128)(2,1)S(1)}, u32[]{:S(2)}, u32[]{:S(2)}) %collective-permute-start.23) | collective-permute-done | bytes 262176 | tf_op jit(solution)/shard_map/ppermute | solution.py:436
  73.0 2.4 %collective-permute-start.17 = (bf16[64,1024]{1,0:T(8,128)(2,1)S(1)}, bf16[64,1024]{1,0:T(8,128)(2,1)S(1)}, u32[]{:S(2)}, u32[]{:S(2)}) collective-permute-start(bf16[64,1024]{1,0:T(8,128)(2,1)S(1)} %get-tuple-element.66), channel_id=1, source_target_pairs={{0,2},{1,3},{2,0},{3,1},{4,6},{5,7},{6,4},{7,5},{8,10},{9,11},{10,... | collective-permute-start | bytes 393224 | tf_op jit(solution)/shard_map/ppermute | solution.py:446
  76.8 2.4 %collective-permute-start.25 = (bf16[64,1024]{1,0:T(8,128)(2,1)S(1)}, bf16[64,1024]{1,0:T(8,128)(2,1)S(1)}, u32[]{:S(2)}, u32[]{:S(2)}) collective-permute-start(bf16[64,1024]{1,0:T(8,128)(2,1)S(1)} %get-tuple-element.82), channel_id=1, source_target_pairs={{0,2},{1,3},{2,0},{3,1},{4,6},{5,7},{6,4},{7,5},{8,10},{9,11},{10,... | collective-permute-start | bytes 393224 | tf_op jit(solution)/shard_map/ppermute | solution.py:446
  79.2 3.9 %collective-permute-done.27 = f32[16,128]{1,0:T(8,128)S(1)} collective-permute-done((f32[16,128]{1,0:T(8,128)S(1)}, f32[16,128]{1,0:T(8,128)S(1)}, u32[]{:S(2)}, u32[]{:S(2)}) %collective-permute-start.27) | collective-permute-done | bytes 8224 | tf_op jit(solution)/shard_map/ppermute | solution.py:507
  83.4 2.0 %collective-permute-start.28 = (f32[8,128]{1,0:T(8,128)S(1)}, f32[8,128]{1,0:T(8,128)S(1)}, u32[]{:S(2)}, u32[]{:S(2)}) collective-permute-start(f32[8,128]{1,0:T(8,128)S(1)} %shard_map.144), channel_id=1, source_target_pairs={{0,8},{4,12},{8,0},{12,4},{1,9},{5,13},{9,1},{13,5},{2,10},{6,14},... | collective-permute-start | bytes 12296 | tf_op jit(solution)/shard_map/ppermute | solution.py:513
  85.4 1.7 %collective-permute-done.28 = f32[8,128]{1,0:T(8,128)S(1)} collective-permute-done((f32[8,128]{1,0:T(8,128)S(1)}, f32[8,128]{1,0:T(8,128)S(1)}, u32[]{:S(2)}, u32[]{:S(2)}) %collective-permute-start.28) | collective-permute-done | bytes 4128 | tf_op jit(solution)/shard_map/ppermute | solution.py:513
  87.1 1.2 %collective-permute-done.29 = f32[8,128]{1,0:T(8,128)S(1)} collective-permute-done((f32[8,128]{1,0:T(8,128)S(1)}, f32[8,128]{1,0:T(8,128)S(1)}, u32[]{:S(2)}, u32[]{:S(2)}) %collective-permute-start.29) | collective-permute-done | bytes 4128 | tf_op jit(solution)/shard_map/ppermute | solution.py:513
  88.8 2.0 %collective-permute-done.25.refs_11_ = bf16[64,1024]{1,0:T(8,128)(2,1)S(1)} collective-permute-done((bf16[64,1024]{1,0:T(8,128)(2,1)S(1)}, bf16[64,1024]{1,0:T(8,128)(2,1)S(1)}, u32[]{:S(2)}, u32[]{:S(2)}) %collective-permute-start.25) | collective-permute-done | bytes 131104 | tf_op jit(solution)/shard_map/ppermute | solution.py:446
  90.9 1.8 %shard_map.143 = bf16[128,2048]{1,0:T(8,128)(2,1)} custom-call(f32[64,1024]{1,0:T(8,128)S(1)} %get-tuple-element.91.refs_0_, bf16[128,1024]{1,0:T(8,128)(2,1)S(1)} %collective-permute-done.16.refs_1_, bf16[64,1024]{1,0:T(8,128)(2,1)S(1)} %collective-permute-done.17.refs_2_, f32[64,1024]{1,0:T(8,128)S(1)} %get-tuple-element.90.refs_3_, ...), custom_call_target="tpu_custom_call" | custom-call | flops 251658 | bytes 31457 | tf_op jit(solution)/shard_map/pallas_call | solution.py:370
  (63 shorter events, 16.4 us)
Async XLA Ops:
  1.7 9.3 %collective-permute-start.1 = (bf16[2,64,1024]{2,1,0:T(8,128)(2,1)S(1)}, bf16[2,64,1024]{2,1,0:T(8,128)(2,1)S(1)}, u32[]{:S(2)}, u32[]{:S(2)}) collective-permute-start(bf16[2,64,1024]{2,1,0:T(8,128)(2,1)S(1)} %get-tuple-element.94.refs_0_), channel_id=1, source_target_pairs={{0,8},{4,12},{8,0},{12,4},{1,9},{5,13},{9,1},{13,5},{2,10},{6,14},... | collective-permute-start | bytes 786440 | tf_op jit(solution)/shard_map/ppermute | solution.py:417
  4.7 8.1 %collective-permute-start = (bf16[2,64,1024]{2,1,0:T(8,128)(2,1)S(1)}, bf16[2,64,1024]{2,1,0:T(8,128)(2,1)S(1)}, u32[]{:S(2)}, u32[]{:S(2)}) collective-permute-start(bf16[2,64,1024]{2,1,0:T(8,128)(2,1)S(1)} %get-tuple-element.94.refs_0_), channel_id=1, source_target_pairs={{0,4},{4,0},{8,12},{12,8},{1,5},{5,1},{9,13},{13,9},{2,6},{6,2},{1... | collective-permute-start | bytes 786440 | tf_op jit(solution)/shard_map/ppermute | solution.py:417
  11.0 1.8 %collective-permute-start.2 = (bf16[2,64,1024]{2,1,0:T(8,128)(2,1)S(1)}, bf16[2,64,1024]{2,1,0:T(8,128)(2,1)S(1)}, u32[]{:S(2)}, u32[]{:S(2)}) collective-permute-start(bf16[2,64,1024]{2,1,0:T(8,128)(2,1)S(1)} %collective-permute-done.1.refs_2_), channel_id=1, source_target_pairs={{0,4},{4,0},{8,12},{12,8},{1,5},{5,1},{9,13},{13,9},{2,6},{6,2},{1... | collective-permute-start | bytes 786440 | tf_op jit(solution)/shard_map/ppermute | solution.py:417
  11.4 9.2 %collective-permute-start.4 = (bf16[2,64,1024]{2,1,0:T(8,128)(2,1)S(1)}, bf16[2,64,1024]{2,1,0:T(8,128)(2,1)S(1)}, u32[]{:S(2)}, u32[]{:S(2)}) collective-permute-start(bf16[2,64,1024]{2,1,0:T(8,128)(2,1)S(1)} %get-tuple-element.93.refs_0_.refs_4_), channel_id=1, source_target_pairs={{0,8},{4,12},{8,0},{12,4},{1,9},{5,13},{9,1},{13,5},{2,10},{6,14},... | collective-permute-start | bytes 786440 | tf_op jit(solution)/shard_map/ppermute | solution.py:417
  13.6 16.1 %collective-permute-start.9 = (bf16[256,1024]{1,0:T(8,128)(2,1)S(1)}, bf16[256,1024]{1,0:T(8,128)(2,1)S(1)}, u32[]{:S(2)}, u32[]{:S(2)}) collective-permute-start(bf16[256,1024]{1,0:T(8,128)(2,1)S(1)} %shard_map.131), channel_id=1, source_target_pairs={{0,16},{16,0},{1,17},{17,1},{2,18},{18,2},{3,19},{19,3},{4,20},{20... | collective-permute-start | bytes 1572872 | tf_op jit(solution)/shard_map/ppermute | solution.py:428
  15.2 5.3 %collective-permute-start.5 = (f32[128,256]{1,0:T(8,128)S(1)}, f32[128,256]{1,0:T(8,128)S(1)}, u32[]{:S(2)}, u32[]{:S(2)}) collective-permute-start(f32[128,256]{1,0:T(8,128)S(1)} %get-tuple-element.47), channel_id=1, source_target_pairs={{0,1},{1,0},{2,3},{3,2},{4,5},{5,4},{6,7},{7,6},{8,9},{9,8},{10,11... | collective-permute-start | bytes 393224 | tf_op jit(solution)/shard_map/ppermute | solution.py:466
  16.8 6.5 %collective-permute-start.3 = (bf16[2,64,1024]{2,1,0:T(8,128)(2,1)S(1)}, bf16[2,64,1024]{2,1,0:T(8,128)(2,1)S(1)}, u32[]{:S(2)}, u32[]{:S(2)}) collective-permute-start(bf16[2,64,1024]{2,1,0:T(8,128)(2,1)S(1)} %get-tuple-element.93.refs_0_.refs_4_), channel_id=1, source_target_pairs={{0,4},{4,0},{8,12},{12,8},{1,5},{5,1},{9,13},{13,9},{2,6},{6,2},{1... | collective-permute-start | bytes 786440 | tf_op jit(solution)/shard_map/ppermute | solution.py:417
  20.6 2.8 %collective-permute-start.6 = (bf16[2,64,1024]{2,1,0:T(8,128)(2,1)S(1)}, bf16[2,64,1024]{2,1,0:T(8,128)(2,1)S(1)}, u32[]{:S(2)}, u32[]{:S(2)}) collective-permute-start(bf16[2,64,1024]{2,1,0:T(8,128)(2,1)S(1)} %collective-permute-done.4.refs_2_.refs_6_), channel_id=1, source_target_pairs={{0,4},{4,0},{8,12},{12,8},{1,5},{5,1},{9,13},{13,9},{2,6},{6,2},{1... | collective-permute-start | bytes 786440 | tf_op jit(solution)/shard_map/ppermute | solution.py:417
  20.7 6.9 %collective-permute-start.7 = (f32[64,256]{1,0:T(8,128)S(1)}, f32[64,256]{1,0:T(8,128)S(1)}, u32[]{:S(2)}, u32[]{:S(2)}) collective-permute-start(f32[64,256]{1,0:T(8,128)S(1)} %slice.86), channel_id=1, source_target_pairs={{0,2},{1,3},{2,0},{3,1},{4,6},{5,7},{6,4},{7,5},{8,10},{9,11},{10,... | collective-permute-start | bytes 196616 | tf_op jit(solution)/shard_map/ppermute | solution.py:468
  24.2 19.8 %collective-permute-start.12 = (bf16[256,1024]{1,0:T(8,128)(2,1)S(1)}, bf16[256,1024]{1,0:T(8,128)(2,1)S(1)}, u32[]{:S(2)}, u32[]{:S(2)}) collective-permute-start(bf16[256,1024]{1,0:T(8,128)(2,1)S(1)} %shard_map.132), channel_id=1, source_target_pairs={{0,1},{1,0},{2,3},{3,2},{4,5},{5,4},{6,7},{7,6},{8,9},{9,8},{10,11... | collective-permute-start | bytes 1572872 | tf_op jit(solution)/shard_map/ppermute | solution.py:428
  28.0 4.0 %collective-permute-start.8 = (f32[1,64,128]{2,1,0:T(8,128)S(1)}, f32[1,64,128]{2,1,0:T(8,128)S(1)}, u32[]{:S(2)}, u32[]{:S(2)}) collective-permute-start(f32[1,64,128]{2,1,0:T(8,128)S(1)} %bitcast.11), channel_id=1, source_target_pairs={{0,16},{16,0},{1,17},{17,1},{2,18},{18,2},{3,19},{19,3},{4,20},{20... | collective-permute-start | bytes 98312 | tf_op jit(solution)/shard_map/ppermute | solution.py:480
  32.0 7.9 %collective-permute-start.10 = (f32[2,64,128]{2,1,0:T(8,128)S(1)}, f32[2,64,128]{2,1,0:T(8,128)S(1)}, u32[]{:S(2)}, u32[]{:S(2)}) collective-permute-start(f32[2,64,128]{2,1,0:T(8,128)S(1)} %pad_maximum_fusion.2), channel_id=1, source_target_pairs={{0,1},{1,0},{2,3},{3,2},{4,5},{5,4},{6,7},{7,6},{8,9},{9,8},{10,11... | collective-permute-start | bytes 196616 | tf_op jit(solution)/shard_map/ppermute | solution.py:484
  32.6 14.7 %collective-permute-start.14 = (bf16[256,1024]{1,0:T(8,128)(2,1)S(1)}, bf16[256,1024]{1,0:T(8,128)(2,1)S(1)}, u32[]{:S(2)}, u32[]{:S(2)}) collective-permute-start(bf16[256,1024]{1,0:T(8,128)(2,1)S(1)} %shard_map.134), channel_id=1, source_target_pairs={{0,16},{16,0},{1,17},{17,1},{2,18},{18,2},{3,19},{19,3},{4,20},{20... | collective-permute-start | bytes 1572872 | tf_op jit(solution)/shard_map/ppermute | solution.py:428
  40.0 5.8 %collective-permute-start.11 = (f32[2,64,128]{2,1,0:T(8,128)S(1)}, f32[2,64,128]{2,1,0:T(8,128)S(1)}, u32[]{:S(2)}, u32[]{:S(2)}) collective-permute-start(f32[2,64,128]{2,1,0:T(8,128)S(1)} %fusion), channel_id=1, source_target_pairs={{0,2},{1,3},{2,0},{3,1},{4,6},{5,7},{6,4},{7,5},{8,10},{9,11},{10,... | collective-permute-start | bytes 196616 | tf_op jit(solution)/shard_map/ppermute | solution.py:484
  41.6 11.6 %collective-permute-start.16 = (bf16[128,1024]{1,0:T(8,128)(2,1)S(1)}, bf16[128,1024]{1,0:T(8,128)(2,1)S(1)}, u32[]{:S(2)}, u32[]{:S(2)}) collective-permute-start(bf16[128,1024]{1,0:T(8,128)(2,1)S(1)} %get-tuple-element.65), channel_id=1, source_target_pairs={{0,1},{1,0},{2,3},{3,2},{4,5},{5,4},{6,7},{7,6},{8,9},{9,8},{10,11... | collective-permute-start | bytes 786440 | tf_op jit(solution)/shard_map/ppermute | solution.py:436
  45.8 7.2 %collective-permute-start.13 = (f32[2,64,128]{2,1,0:T(8,128)S(1)}, f32[2,64,128]{2,1,0:T(8,128)S(1)}, u32[]{:S(2)}, u32[]{:S(2)}) collective-permute-start(f32[2,64,128]{2,1,0:T(8,128)S(1)} %fusion.3), channel_id=1, source_target_pairs={{0,8},{4,12},{8,0},{12,4},{1,9},{5,13},{9,1},{13,5},{2,10},{6,14},... | collective-permute-start | bytes 196616 | tf_op jit(solution)/shard_map/ppermute | solution.py:492
  48.3 14.6 %collective-permute-start.18 = (bf16[128,1024]{1,0:T(8,128)(2,1)S(1)}, bf16[128,1024]{1,0:T(8,128)(2,1)S(1)}, u32[]{:S(2)}, u32[]{:S(2)}) collective-permute-start(bf16[128,1024]{1,0:T(8,128)(2,1)S(1)} %get-tuple-element.73), channel_id=1, source_target_pairs={{0,1},{1,0},{2,3},{3,2},{4,5},{5,4},{6,7},{7,6},{8,9},{9,8},{10,11... | collective-permute-start | bytes 786440 | tf_op jit(solution)/shard_map/ppermute | solution.py:436
  49.8 16.4 %collective-permute-start.19 = (bf16[128,1024]{1,0:T(8,128)(2,1)S(1)}, bf16[128,1024]{1,0:T(8,128)(2,1)S(1)}, u32[]{:S(2)}, u32[]{:S(2)}) collective-permute-start(bf16[128,1024]{1,0:T(8,128)(2,1)S(1)} %get-tuple-element.74), channel_id=1, source_target_pairs={{0,2},{1,3},{2,0},{3,1},{4,6},{5,7},{6,4},{7,5},{8,10},{9,11},{10,... | collective-permute-start | bytes 786440 | tf_op jit(solution)/shard_map/ppermute | solution.py:436
  52.1 12.5 %collective-permute-start.20 = (bf16[256,1024]{1,0:T(8,128)(2,1)S(1)}, bf16[256,1024]{1,0:T(8,128)(2,1)S(1)}, u32[]{:S(2)}, u32[]{:S(2)}) collective-permute-start(bf16[256,1024]{1,0:T(8,128)(2,1)S(1)} %shard_map.136), channel_id=1, source_target_pairs={{0,16},{16,0},{1,17},{17,1},{2,18},{18,2},{3,19},{19,3},{4,20},{20... | collective-permute-start | bytes 1572872 | tf_op jit(solution)/shard_map/ppermute | solution.py:428
  53.0 1.4 %collective-permute-start.15 = (f32[4,64,128]{2,1,0:T(8,128)S(1)}, f32[4,64,128]{2,1,0:T(8,128)S(1)}, u32[]{:S(2)}, u32[]{:S(2)}) collective-permute-start(f32[4,64,128]{2,1,0:T(8,128)S(1)} %pad_maximum_fusion.1), channel_id=1, source_target_pairs={{0,4},{4,0},{8,12},{12,8},{1,5},{5,1},{9,13},{13,9},{2,6},{6,2},{1... | collective-permute-start | bytes 393224 | tf_op jit(solution)/shard_map/ppermute | solution.py:492
  61.8 4.4 %collective-permute-start.24 = (f32[16,512]{1,0:T(8,128)S(1)}, f32[16,512]{1,0:T(8,128)S(1)}, u32[]{:S(2)}, u32[]{:S(2)}) collective-permute-start(f32[16,512]{1,0:T(8,128)S(1)} %slice.92), channel_id=1, source_target_pairs={{0,16},{16,0},{1,17},{17,1},{2,18},{18,2},{3,19},{19,3},{4,20},{20... | collective-permute-start | bytes 98312 | tf_op jit(solution)/shard_map/ppermute | solution.py:507
  65.5 6.7 %collective-permute-start.23 = (bf16[128,1024]{1,0:T(8,128)(2,1)S(1)}, bf16[128,1024]{1,0:T(8,128)(2,1)S(1)}, u32[]{:S(2)}, u32[]{:S(2)}) collective-permute-start(bf16[128,1024]{1,0:T(8,128)(2,1)S(1)} %get-tuple-element.80), channel_id=1, source_target_pairs={{0,1},{1,0},{2,3},{3,2},{4,5},{5,4},{6,7},{7,6},{8,9},{9,8},{10,11... | collective-permute-start | bytes 786440 | tf_op jit(solution)/shard_map/ppermute | solution.py:436
  66.3 6.1 %collective-permute-start.26 = (f32[16,256]{1,0:T(8,128)S(1)}, f32[16,256]{1,0:T(8,128)S(1)}, u32[]{:S(2)}, u32[]{:S(2)}) collective-permute-start(f32[16,256]{1,0:T(8,128)S(1)} %slice.94), channel_id=1, source_target_pairs={{0,1},{1,0},{2,3},{3,2},{4,5},{5,4},{6,7},{7,6},{8,9},{9,8},{10,11... | collective-permute-start | bytes 49160 | tf_op jit(solution)/shard_map/ppermute | solution.py:507
  72.4 10.6 %collective-permute-start.27 = (f32[16,128]{1,0:T(8,128)S(1)}, f32[16,128]{1,0:T(8,128)S(1)}, u32[]{:S(2)}, u32[]{:S(2)}) collective-permute-start(f32[16,128]{1,0:T(8,128)S(1)} %slice.96), channel_id=1, source_target_pairs={{0,2},{1,3},{2,0},{3,1},{4,6},{5,7},{6,4},{7,5},{8,10},{9,11},{10,... | collective-permute-start | bytes 24584 | tf_op jit(solution)/shard_map/ppermute | solution.py:507
  73.0 15.8 %collective-permute-start.17 = (bf16[64,1024]{1,0:T(8,128)(2,1)S(1)}, bf16[64,1024]{1,0:T(8,128)(2,1)S(1)}, u32[]{:S(2)}, u32[]{:S(2)}) collective-permute-start(bf16[64,1024]{1,0:T(8,128)(2,1)S(1)} %get-tuple-element.66), channel_id=1, source_target_pairs={{0,2},{1,3},{2,0},{3,1},{4,6},{5,7},{6,4},{7,5},{8,10},{9,11},{10,... | collective-permute-start | bytes 393224 | tf_op jit(solution)/shard_map/ppermute | solution.py:446
  75.4 13.5 %collective-permute-start.21 = (bf16[64,1024]{1,0:T(8,128)(2,1)S(1)}, bf16[64,1024]{1,0:T(8,128)(2,1)S(1)}, u32[]{:S(2)}, u32[]{:S(2)}) collective-permute-start(bf16[64,1024]{1,0:T(8,128)(2,1)S(1)} %get-tuple-element.79), channel_id=1, source_target_pairs={{0,2},{1,3},{2,0},{3,1},{4,6},{5,7},{6,4},{7,5},{8,10},{9,11},{10,... | collective-permute-start | bytes 393224 | tf_op jit(solution)/shard_map/ppermute | solution.py:446
  75.9 12.9 %collective-permute-start.22 = (bf16[64,1024]{1,0:T(8,128)(2,1)S(1)}, bf16[64,1024]{1,0:T(8,128)(2,1)S(1)}, u32[]{:S(2)}, u32[]{:S(2)}) collective-permute-start(bf16[64,1024]{1,0:T(8,128)(2,1)S(1)} %get-tuple-element.78), channel_id=1, source_target_pairs={{0,16},{16,0},{1,17},{17,1},{2,18},{18,2},{3,19},{19,3},{4,20},{20... | collective-permute-start | bytes 393224 | tf_op jit(solution)/shard_map/ppermute | solution.py:446
  76.8 14.1 %collective-permute-start.25 = (bf16[64,1024]{1,0:T(8,128)(2,1)S(1)}, bf16[64,1024]{1,0:T(8,128)(2,1)S(1)}, u32[]{:S(2)}, u32[]{:S(2)}) collective-permute-start(bf16[64,1024]{1,0:T(8,128)(2,1)S(1)} %get-tuple-element.82), channel_id=1, source_target_pairs={{0,2},{1,3},{2,0},{3,1},{4,6},{5,7},{6,4},{7,5},{8,10},{9,11},{10,... | collective-permute-start | bytes 393224 | tf_op jit(solution)/shard_map/ppermute | solution.py:446
  83.4 3.6 %collective-permute-start.28 = (f32[8,128]{1,0:T(8,128)S(1)}, f32[8,128]{1,0:T(8,128)S(1)}, u32[]{:S(2)}, u32[]{:S(2)}) collective-permute-start(f32[8,128]{1,0:T(8,128)S(1)} %shard_map.144), channel_id=1, source_target_pairs={{0,8},{4,12},{8,0},{12,4},{1,9},{5,13},{9,1},{13,5},{2,10},{6,14},... | collective-permute-start | bytes 12296 | tf_op jit(solution)/shard_map/ppermute | solution.py:513
  87.1 1.2 %collective-permute-start.29 = (f32[8,128]{1,0:T(8,128)S(1)}, f32[8,128]{1,0:T(8,128)S(1)}, u32[]{:S(2)}, u32[]{:S(2)}) collective-permute-start(f32[8,128]{1,0:T(8,128)S(1)} %add.54), channel_id=1, source_target_pairs={{0,4},{4,0},{8,12},{12,8},{1,5},{5,1},{9,13},{13,9},{2,6},{6,2},{1... | collective-permute-start | bytes 12296 | tf_op jit(solution)/shard_map/ppermute | solution.py:513

commit v3 on v2

--- a/solution.py
+++ b/solution.py
@@ -201,7 +201,7 @@
 
 def update(scale, me, gram, left, right):
     rows, cols = gram.shape
-    tile = min(rows, 256)
+    tile = min(rows, 512)
     deep = left.shape[0]
     return pl.pallas_call(
         functools.partial(update_kernel, scale),
@@ -246,7 +246,7 @@
     count, unit, depth = rows.shape
     sort_rows(me[0], sizes, direct, bits, first, count, cans, rows)
     width = low.shape[1]
-    tile = min(width, 512)
+    tile = next(tile for tile in (512, 256, 128) if width % tile == 0)
     for at in range(0, width, tile):
         value = dot(
             rows[...].reshape(count * unit, depth),
@@ -352,11 +352,11 @@
 
 def finish_kernel(seqs, scale, norm, spots, *refs):
     terms, (thin, col, mapped) = list(refs[:-3]), refs[-3:]
-    for number, row, column, rows, width in spots:
+    for offsets, row, column, rows, width in spots:
         value = 0.0
-        for _ in range(number):
+        for offset in offsets:
             term = terms.pop(0)
-            value = value + term[term.shape[0] - rows :, :].astype(jnp.float32)
+            value = value + term[term.shape[0] - rows :, offset : offset + width].astype(jnp.float32)
         share = dot(thin[:seqs, row : row + rows], col[:, column : column + width], TN, lax.Precision.HIGHEST)
         mapped[row : row + rows, column : column + width] = ((value + share * scale) * norm).astype(jnp.bfloat16)
 
@@ -365,8 +365,8 @@
     seqs, cols = col.shape
     spots, args = [], []
     for terms, row, column, rows, width in kept:
-        spots.append((len(terms), row, column, rows, width))
-        args += terms
+        spots.append(([offset for _, offset in terms], row, column, rows, width))
+        args += [term for term, _ in terms]
     return pl.pallas_call(
         functools.partial(finish_kernel, seqs, scale, norm, spots),
         out_shape=jax.ShapeDtypeStruct((chunk, cols), jnp.bfloat16),
@@ -435,15 +435,19 @@
         axis, size, bit, _ = steps[1]
         return keep, [lax.ppermute(low, axis, pairs(size, bit))]
 
-    def add_next(steps, keep, arrived, gate):
-        left_over = 1 << (len(steps) - 1 - len(arrived))
+    def add_next(steps, pieces, gate):
+        left_over = 1 << (len(steps) - 1 - len(pieces[0][1]))
         rows = (left_over // 2) * half_rows
-        low = keep[:rows]
-        for array in arrived:
-            low = low + array[-left_over * half_rows :][:rows].astype(jnp.float32)
-        low = after(low.astype(jnp.bfloat16), gate)
-        axis, size, bit, _ = steps[len(arrived) + 1]
-        return low, keep[rows:], [*arrived, lax.ppermute(low, axis, pairs(size, bit))]
+        lows, rest = [], []
+        for keep, arrived in pieces:
+            low = keep[:rows]
+            for array in arrived:
+                low = low + array[-left_over * half_rows :][:rows].astype(jnp.float32)
+            lows.append(low.astype(jnp.bfloat16))
+            rest.append((keep[rows:], arrived))
+        low = after(jnp.concatenate(lows, axis=1) if lows[1:] else lows[0], gate)
+        axis, size, bit, _ = steps[len(pieces[0][1]) + 1]
+        return low, rest, lax.ppermute(low, axis, pairs(size, bit))
 
     if direct:
         own = canaries.reshape(-1, 2, half_rows, depth)
@@ -459,65 +463,73 @@
     )
     halves = [spread_canaries(own[:, 0], gram_low) if direct else [own[:, 0]]]
     middle = cols_here // 2
+    split = cols_here // 2
     low_a = begin(0, grp_first, 0, middle, gram_low)
     recv_a = send(grp_first, low_a)
-    gate = low_a
+    low_d = begin(0, grp_first, middle, middle, low_a)
+    gate = low_d
     for axis, size, bit, _ in steps_mp[:-1]:
         token_sums = token_sums[-sent.shape[0] :] + after(lax.ppermute(sent, axis, pairs(size, bit)), gate)
         sent = token_sums[: token_sums.shape[0] // 2]
     there = lax.ppermute(sent, "mp", pairs(mp, steps_mp[-1][2]))
     halves.append(spread_canaries(own[:, 1], token_sums) if direct else [own[:, 1]])
-    low_c = begin(1, mp_first, middle, middle, token_sums)
+    low_c = begin(1, mp_first, split, cols_here - split, token_sums)
     recv_c = send(mp_first, low_c)
     row = feature_rows(1.0 / math.sqrt(seq_len), rank, token_sums, after(there, low_c))[None]
 
     gathered = row
-    low_d = begin(0, grp_first, middle, middle, row)
-    recv_d = send(grp_first, low_d)
-    keep_a, there_a = add_first(0, grp_first, 0, middle, recv_a, low_d)
+    recv_d = send(grp_first, after(low_d, row))
+    low_b = begin(1, grp_first, 0, split, row)
+    keep_a, there_a = add_first(0, grp_first, 0, middle, recv_a, low_b)
     gate = keep_a
     for bit in bits_of(grp):
         gathered = jnp.concatenate([gathered, after(lax.ppermute(gathered, "grp", pairs(grp, bit)), gate)])
-    low_b = begin(1, grp_first, 0, middle, gathered)
-    gate = low_b
     for at, bit in enumerate(reversed(bits_of(mp))):
         gathered = gathered + after(lax.ppermute(gathered, "mp", pairs(mp, bit)), gate)
         if at == 0:
-            keep_c, there_c = add_first(1, mp_first, middle, middle, recv_c, gathered)
+            recv_b = send(grp_first, after(low_b, gathered))
+            keep_c, there_c = add_first(1, mp_first, split, cols_here - split, recv_c, gathered)
             gate = keep_c
-    recv_b = send(grp_first, after(low_b, gathered))
     keep_d, there_d = add_first(0, grp_first, middle, middle, recv_d, gathered)
     gate = keep_d
     for bit in bits_of(dp):
         gathered = jnp.concatenate([gathered, after(lax.ppermute(gathered, "dp", pairs(dp, bit)), gate)])
-        if bit == bits_of(dp)[0]:
-            low_a, keep_a, there_a = add_next(grp_first, keep_a, there_a, gathered)
-            gate = low_a
     left, right, col = spread(me, gathered, dp, mp, rows_here, cols_here)
     thin = thin_products(
         sizes, direct, [code for _, _, _, code in grp_first], me, halves, gram_low, left, col
     )
-    gram_new = update(scale, after(me, thin), gram_here, left, right)
-    keep_b, there_b = add_first(1, grp_first, 0, middle, recv_b, gram_new)
-    low_c, keep_c, there_c = add_next(mp_first, keep_c, there_c, keep_b)
-    low_d, keep_d, there_d = add_next(grp_first, keep_d, there_d, low_c)
-    gate = low_d
+    low_a, ((keep_a, there_a), (keep_d, there_d)), last_a = add_next(
+        grp_first, [(keep_a, there_a), (keep_d, there_d)], thin
+    )
+    keep_b, there_b = add_first(1, grp_first, 0, split, recv_b, low_a)
+    gate = keep_b
     for at, (axis, size, bit, _) in enumerate(grp_first):
         half = thin.shape[1] // 2
         thin = thin[:, half:] + after(lax.ppermute(thin[:, :half], axis, pairs(size, bit)), gate)
         if at == 0:
-            low_b, keep_b, there_b = add_next(grp_first, keep_b, there_b, thin)
+            gram_new = update(scale, after(me, thin), gram_here, left, right)
+            low_c, ((keep_c, there_c),), last_c = add_next(mp_first, [(keep_c, there_c)], gram_new)
+            low_b, ((keep_b, there_b),), last_b = add_next(grp_first, [(keep_b, there_b)], low_c)
             gate = low_b
+        elif at == 1:
+            last_a = after(last_a, after(low_b, thin)).astype(jnp.float32)
+            sum_a = [
+                keep + there[0][-half_rows:].astype(jnp.float32) + last_a[:, at : at + middle]
+                for keep, there, at in ((keep_a, there_a, 0), (keep_d, there_d, middle))
+            ]
+            gate = sum_a[0]
     scores = score(scale, norm * norm, thin, col)
-    for bit in bits_of(dp):
-        scores = scores + lax.ppermute(scores, "dp", pairs(dp, bit))
+    whole = lambda keep, arrived, last: [(keep, 0), *((array, 0) for array in arrived), (last, 0)]
     kept = [
-        ([keep_a, *there_a], 0, 0, half_rows, middle),
-        ([keep_d, *there_d], 0, middle, half_rows, middle),
-        ([keep_c, *there_c], half_rows, middle, half_rows, middle),
-        ([keep_b, *there_b], half_rows, 0, half_rows, middle),
+        ([(sum_a[0], 0)], 0, 0, half_rows, middle),
+        ([(sum_a[1], 0)], 0, middle, half_rows, middle),
+        (whole(keep_c, there_c, last_c), half_rows, split, half_rows, cols_here - split),
+        (whole(keep_b, there_b, last_b), half_rows, 0, half_rows, split),
     ]
     mapped = finish(scale, norm, kept, thin, col, chunk)
+    gate = mapped
+    for bit in bits_of(dp):
+        scores = scores + after(lax.ppermute(scores, "dp", pairs(dp, bit)), gate)
     return gram_new, mapped, scores
 
 

time: 92.9 us -> 88 us (0.947)
  waiting for transfers between devices: 30 us -> 26.9 us
  starting transfers between devices: 37 us -> 35.2 us
    ppermute x6 -> x5, starting transfers between devices: 8.15 us -> 4.61 us  [the longest x3 3.19 us: add_next(): return (low, rest, lax.ppermute(low, axis, pairs(size, bit)))]
    ppermute x4, waiting for transfers between devices: 4.5 us -> 6.73 us  [add_first(): return (keep, [lax.ppermute(low, axis, pairs(size, bit))])]
    ppermute x6 -> x5, waiting for transfers between devices: 4.88 us -> 2.72 us  [the longest x3 1.49 us: add_next(): return (low, rest, lax.ppermute(low, axis, pairs(size, bit)))]
    ppermute x4, starting transfers between devices: 6.95 us -> 8.77 us  [add_first(): return (keep, [lax.ppermute(low, axis, pairs(size, bit))])]
    ppermute x4, waiting for transfers between devices: 1.63 us -> 0.01 us  [send(): return lax.ppermute(low, axis, pairs(size, bit))]
    ppermute x3, waiting for transfers between devices: 3.98 us -> 2.37 us  [shards(): lax.ppermute(thin[:, :half], axis, pairs(size, bit))]
  transfers between devices with their start and end apart: 30 -> 29, of which waited for: 14 -> 16; matrix products, arithmetic and copies ran while one was open for 1% -> 0% of each run, Pallas kernels for 23% -> 26%
where the time goes in v3:
time: 88 us; the launch traced here: 87.9 us
  starting transfers between devices  35.2 us (40%)
  waiting for transfers between devices  26.9 us (31%)
  Pallas kernels  22.8 us (26%)
  local copies, waits for them, and re-layouts  1.09 us (1%)
  other arithmetic  1.01 us (1%)
    ppermute x4, starting transfers between devices, add_first(): return (keep, [lax.ppermute(low, axis, pairs(size, bit))])  8.77 us
    ppermute x2, waiting for transfers between devices, shards(): lax.ppermute(gathered, 'mp', pairs(mp, bit))  7.41 us
    pallas_call x8, Pallas kernels, product(): pl.pallas_call(functools.partial(product_kernel, sizes, direct, bits, fir...  6.88 us
    ppermute x4, waiting for transfers between devices, add_first(): return (keep, [lax.ppermute(low, axis, pairs(size, bit))])  6.73 us
    pallas_call x1, Pallas kernels, project_all(): pl.pallas_call(functools.partial(project_kernel, order, tile), out_shape=...  6.08 us
    ppermute x4, starting transfers between devices, send(): return lax.ppermute(low, axis, pairs(size, bit))  5.09 us
    ppermute x6, starting transfers between devices, spread_canaries(): lax.ppermute(block, 'dp', pairs(dp, bit))  4.85 us
    pallas_call x1, Pallas kernels, update(): pl.pallas_call(functools.partial(update_kernel, scale), out_shape=jax.Sha...  4.17 us
  transfers between devices with their start and end apart: 29, of which 16 were waited for; matrix products, arithmetic and copies ran while one was open for 0% of the time, Pallas kernels for 26%

profile of v3, /device:TPU:0, one launch (start us, length us, event | category | flops | bytes accessed | tf_op | source)
XLA Modules:
  0.0 87.9 jit_solution(17356494940370202649)
XLA Ops:
  0.6 1.1 %slice_bitcast_fusion = (bf16[2,64,1024]{2,1,0:T(8,128)(2,1)S(1)}, bf16[2,64,1024]{2,1,0:T(8,128)(2,1)S(1)}) fusion(bf16[2,2,64,1024]{3,2,1,0:T(8,128)(2,1)} %bitcast.15), kind=kLoop, calls=%fused_computation.2 | loop fusion | bytes 1048576 | tf_op jit(solution)/shard_map/squeeze | solution.py:475
  1.7 3.0 %collective-permute-start.1 = (bf16[2,64,1024]{2,1,0:T(8,128)(2,1)S(1)}, bf16[2,64,1024]{2,1,0:T(8,128)(2,1)S(1)}, u32[]{:S(2)}, u32[]{:S(2)}) collective-permute-start(bf16[2,64,1024]{2,1,0:T(8,128)(2,1)S(1)} %get-tuple-element.96.refs_0_), channel_id=1, source_target_pairs={{0,8},{4,12},{8,0},{12,4},{1,9},{5,13},{9,1},{13,5},{2,10},{6,14},... | collective-permute-start | bytes 786440 | tf_op jit(solution)/shard_map/ppermute | solution.py:417
  4.7 6.1 %shard_map.130 = (f32[128,256]{1,0:T(8,128)S(1)}, f32[128,256]{1,0:T(8,128)S(1)}, f32[1024,2048]{1,0:T(8,128)S(1)}, bf16[1024,2048]{1,0:T(8,128)(2,1)S(1)}) custom-call(s32[1]{0:T(128)} %bitcast.me, bf16[1,256,1024]{2,1,0:T(8,128)(2,1)} %refs_0_.1, bf16[1,256,3584]{2,1,0:T(8,128)(2,1)} %refs_1_.1, bf16[1,256,3584]{2,1,0:T(8,128)(2,1)} %refs_2_.1, ...), custom_call_target="tpu_custom_call" | custom-call | flops 3019898 | bytes 65536 | tf_op jit(solution)/shard_map/pallas_call | solution.py:99
  11.4 1.4 %collective-permute-start.4 = (bf16[2,64,1024]{2,1,0:T(8,128)(2,1)S(1)}, bf16[2,64,1024]{2,1,0:T(8,128)(2,1)S(1)}, u32[]{:S(2)}, u32[]{:S(2)}) collective-permute-start(bf16[2,64,1024]{2,1,0:T(8,128)(2,1)S(1)} %get-tuple-element.95.refs_0_.refs_4_), channel_id=1, source_target_pairs={{0,8},{4,12},{8,0},{12,4},{1,9},{5,13},{9,1},{13,5},{2,10},{6,14},... | collective-permute-start | bytes 786440 | tf_op jit(solution)/shard_map/ppermute | solution.py:417
  13.6 1.6 %collective-permute-start.9 = (bf16[256,1024]{1,0:T(8,128)(2,1)S(1)}, bf16[256,1024]{1,0:T(8,128)(2,1)S(1)}, u32[]{:S(2)}, u32[]{:S(2)}) collective-permute-start(bf16[256,1024]{1,0:T(8,128)(2,1)S(1)} %shard_map.131), channel_id=1, source_target_pairs={{0,16},{16,0},{1,17},{17,1},{2,18},{18,2},{3,19},{19,3},{4,20},{20... | collective-permute-start | bytes 1572872 | tf_op jit(solution)/shard_map/ppermute | solution.py:428
  15.2 1.6 %collective-permute-start.5 = (f32[128,256]{1,0:T(8,128)S(1)}, f32[128,256]{1,0:T(8,128)S(1)}, u32[]{:S(2)}, u32[]{:S(2)}) collective-permute-start(f32[128,256]{1,0:T(8,128)S(1)} %get-tuple-element.49), channel_id=1, source_target_pairs={{0,1},{1,0},{2,3},{3,2},{4,5},{5,4},{6,7},{7,6},{8,9},{9,8},{10,11... | collective-permute-start | bytes 393224 | tf_op jit(solution)/shard_map/ppermute | solution.py:472
  17.6 3.0 %collective-permute-done.5 = f32[128,256]{1,0:T(8,128)S(1)} collective-permute-done((f32[128,256]{1,0:T(8,128)S(1)}, f32[128,256]{1,0:T(8,128)S(1)}, u32[]{:S(2)}, u32[]{:S(2)}) %collective-permute-start.5) | collective-permute-done | bytes 131104 | tf_op jit(solution)/shard_map/ppermute | solution.py:472
  20.7 2.7 %collective-permute-start.7 = (f32[64,256]{1,0:T(8,128)S(1)}, f32[64,256]{1,0:T(8,128)S(1)}, u32[]{:S(2)}, u32[]{:S(2)}) collective-permute-start(f32[64,256]{1,0:T(8,128)S(1)} %slice.102), channel_id=1, source_target_pairs={{0,2},{1,3},{2,0},{3,1},{4,6},{5,7},{6,4},{7,5},{8,10},{9,11},{10,... | collective-permute-start | bytes 196616 | tf_op jit(solution)/shard_map/ppermute | solution.py:474
  24.2 1.7 %collective-permute-start.12 = (bf16[256,1024]{1,0:T(8,128)(2,1)S(1)}, bf16[256,1024]{1,0:T(8,128)(2,1)S(1)}, u32[]{:S(2)}, u32[]{:S(2)}) collective-permute-start(bf16[256,1024]{1,0:T(8,128)(2,1)S(1)} %shard_map.133), channel_id=1, source_target_pairs={{0,1},{1,0},{2,3},{3,2},{4,5},{5,4},{6,7},{7,6},{8,9},{9,8},{10,11... | collective-permute-start | bytes 1572872 | tf_op jit(solution)/shard_map/ppermute | solution.py:428
  25.9 1.7 %collective-permute-done.7.there = f32[64,256]{1,0:T(8,128)S(1)} collective-permute-done((f32[64,256]{1,0:T(8,128)S(1)}, f32[64,256]{1,0:T(8,128)S(1)}, u32[]{:S(2)}, u32[]{:S(2)}) %collective-permute-start.7) | collective-permute-done | bytes 65568 | tf_op jit(solution)/shard_map/ppermute | solution.py:474
  30.6 1.4 %collective-permute-done.8 = f32[1,64,128]{2,1,0:T(8,128)S(1)} collective-permute-done((f32[1,64,128]{2,1,0:T(8,128)S(1)}, f32[1,64,128]{2,1,0:T(8,128)S(1)}, u32[]{:S(2)}, u32[]{:S(2)}) %collective-permute-start.8) | collective-permute-done | bytes 32800 | tf_op jit(solution)/shard_map/ppermute | solution.py:486
  33.4 6.5 %collective-permute-done.10 = f32[2,64,128]{2,1,0:T(8,128)S(1)} collective-permute-done((f32[2,64,128]{2,1,0:T(8,128)S(1)}, f32[2,64,128]{2,1,0:T(8,128)S(1)}, u32[]{:S(2)}, u32[]{:S(2)}) %collective-permute-start.10) | collective-permute-done | bytes 65568 | tf_op jit(solution)/shard_map/ppermute | solution.py:488
  40.0 1.6 %collective-permute-start.11 = (f32[2,64,128]{2,1,0:T(8,128)S(1)}, f32[2,64,128]{2,1,0:T(8,128)S(1)}, u32[]{:S(2)}, u32[]{:S(2)}) collective-permute-start(f32[2,64,128]{2,1,0:T(8,128)S(1)} %fusion), channel_id=1, source_target_pairs={{0,2},{1,3},{2,0},{3,1},{4,6},{5,7},{6,4},{7,5},{8,10},{9,11},{10,... | collective-permute-start | bytes 196616 | tf_op jit(solution)/shard_map/ppermute | solution.py:488
  41.6 2.5 %collective-permute-start.17 = (bf16[128,1024]{1,0:T(8,128)(2,1)S(1)}, bf16[128,1024]{1,0:T(8,128)(2,1)S(1)}, u32[]{:S(2)}, u32[]{:S(2)}) collective-permute-start(bf16[128,1024]{1,0:T(8,128)(2,1)S(1)} %get-tuple-element.71), channel_id=1, source_target_pairs={{0,1},{1,0},{2,3},{3,2},{4,5},{5,4},{6,7},{7,6},{8,9},{9,8},{10,11... | collective-permute-start | bytes 786440 | tf_op jit(solution)/shard_map/ppermute | solution.py:436
  45.8 1.5 %collective-permute-start.13 = (f32[2,64,128]{2,1,0:T(8,128)S(1)}, f32[2,64,128]{2,1,0:T(8,128)S(1)}, u32[]{:S(2)}, u32[]{:S(2)}) collective-permute-start(f32[2,64,128]{2,1,0:T(8,128)S(1)} %fusion.1), channel_id=1, source_target_pairs={{0,8},{4,12},{8,0},{12,4},{1,9},{5,13},{9,1},{13,5},{2,10},{6,14},... | collective-permute-start | bytes 196616 | tf_op jit(solution)/shard_map/ppermute | solution.py:496
  49.2 1.4 %collective-permute-start.18 = (bf16[128,1024]{1,0:T(8,128)(2,1)S(1)}, bf16[128,1024]{1,0:T(8,128)(2,1)S(1)}, u32[]{:S(2)}, u32[]{:S(2)}) collective-permute-start(bf16[128,1024]{1,0:T(8,128)(2,1)S(1)} %get-tuple-element.72), channel_id=1, source_target_pairs={{0,1},{1,0},{2,3},{3,2},{4,5},{5,4},{6,7},{7,6},{8,9},{9,8},{10,11... | collective-permute-start | bytes 786440 | tf_op jit(solution)/shard_map/ppermute | solution.py:436
  50.5 2.4 %collective-permute-start.21 = (bf16[128,1024]{1,0:T(8,128)(2,1)S(1)}, bf16[128,1024]{1,0:T(8,128)(2,1)S(1)}, u32[]{:S(2)}, u32[]{:S(2)}) collective-permute-start(bf16[128,1024]{1,0:T(8,128)(2,1)S(1)} %get-tuple-element.81), channel_id=1, source_target_pairs={{0,2},{1,3},{2,0},{3,1},{4,6},{5,7},{6,4},{7,5},{8,10},{9,11},{10,... | collective-permute-start | bytes 786440 | tf_op jit(solution)/shard_map/ppermute | solution.py:436
  53.1 1.3 %collective-permute-done.15 = f32[4,64,128]{2,1,0:T(8,128)S(1)} collective-permute-done((f32[4,64,128]{2,1,0:T(8,128)S(1)}, f32[4,64,128]{2,1,0:T(8,128)S(1)}, u32[]{:S(2)}, u32[]{:S(2)}) %collective-permute-start.15) | collective-permute-done | bytes 131104 | tf_op jit(solution)/shard_map/ppermute | solution.py:496
  54.5 2.9 %shard_map.140 = f32[16,1024]{1,0:T(8,128)S(1)} custom-call(s32[1]{0:T(128)} %bitcast.me, bf16[2,64,1024]{2,1,0:T(8,128)(2,1)S(1)} %get-tuple-element.96.refs_0_, bf16[2,64,1024]{2,1,0:T(8,128)(2,1)S(1)} %collective-permute-done.refs_1_, bf16[2,64,1024]{2,1,0:T(8,128)(2,1)S(1)} %collective-permute-done.1.refs_2_, ...), custom_call_target="tpu_custom_call" | custom-call | flops 8053063 | bytes 62914 | tf_op jit(solution)/shard_map/pallas_call | solution.py:325
  58.5 3.3 %collective-permute-done.18 = bf16[128,1024]{1,0:T(8,128)(2,1)S(1)} collective-permute-done((bf16[128,1024]{1,0:T(8,128)(2,1)S(1)}, bf16[128,1024]{1,0:T(8,128)(2,1)S(1)}, u32[]{:S(2)}, u32[]{:S(2)}) %collective-permute-start.18) | collective-permute-done | bytes 262176 | tf_op jit(solution)/shard_map/ppermute | solution.py:436
  63.1 2.5 %collective-permute-start.23 = (bf16[128,1024]{1,0:T(8,128)(2,1)S(1)}, bf16[128,1024]{1,0:T(8,128)(2,1)S(1)}, u32[]{:S(2)}, u32[]{:S(2)}) collective-permute-start(bf16[128,1024]{1,0:T(8,128)(2,1)S(1)} %get-tuple-element.83), channel_id=1, source_target_pairs={{0,1},{1,0},{2,3},{3,2},{4,5},{5,4},{6,7},{7,6},{8,9},{9,8},{10,11... | collective-permute-start | bytes 786440 | tf_op jit(solution)/shard_map/ppermute | solution.py:436
  65.7 2.0 %collective-permute-done.21.refs_3_ = bf16[128,1024]{1,0:T(8,128)(2,1)S(1)} collective-permute-done((bf16[128,1024]{1,0:T(8,128)(2,1)S(1)}, bf16[128,1024]{1,0:T(8,128)(2,1)S(1)}, u32[]{:S(2)}, u32[]{:S(2)}) %collective-permute-start.21) | collective-permute-done | bytes 262176 | tf_op jit(solution)/shard_map/ppermute | solution.py:436
  67.8 4.2 %shard_map.142 = f32[1024,2048]{1,0:T(8,128)} custom-call(s32[1]{0:T(128)} %bitcast.me, f32[1024,2048]{1,0:T(8,128)S(1)} %get-tuple-element.79.gram, bf16[32,1024]{1,0:T(8,128)(2,1)S(1)} %get-tuple-element.69.refs_9_.left, bf16[32,2048]{1,0:T(8,128)(2,1)S(1)} %get-tuple-element.80.right), custom_call_target="tpu_custom_call" | custom-call | flops 1342177 | bytes 167772 | tf_op jit(solution)/shard_map/pallas_call | solution.py:206
  72.6 1.3 %collective-permute-start.22 = (bf16[64,1024]{1,0:T(8,128)(2,1)S(1)}, bf16[64,1024]{1,0:T(8,128)(2,1)S(1)}, u32[]{:S(2)}, u32[]{:S(2)}) collective-permute-start(bf16[64,1024]{1,0:T(8,128)(2,1)S(1)} %get-tuple-element.82), channel_id=1, source_target_pairs={{0,16},{16,0},{1,17},{17,1},{2,18},{18,2},{3,19},{19,3},{4,20},{20... | collective-permute-start | bytes 393224 | tf_op jit(solution)/shard_map/ppermute | solution.py:450
  73.9 1.2 %collective-permute-done.20 = bf16[64,2048]{1,0:T(8,128)(2,1)S(1)} collective-permute-done((bf16[64,2048]{1,0:T(8,128)(2,1)S(1)}, bf16[64,2048]{1,0:T(8,128)(2,1)S(1)}, u32[]{:S(2)}, u32[]{:S(2)}) %collective-permute-start.20) | collective-permute-done | bytes 262176 | tf_op jit(solution)/shard_map/ppermute | solution.py:450
  75.1 1.4 %collective-permute-done.23.refs_6_ = bf16[128,1024]{1,0:T(8,128)(2,1)S(1)} collective-permute-done((bf16[128,1024]{1,0:T(8,128)(2,1)S(1)}, bf16[128,1024]{1,0:T(8,128)(2,1)S(1)}, u32[]{:S(2)}, u32[]{:S(2)}) %collective-permute-start.23) | collective-permute-done | bytes 262176 | tf_op jit(solution)/shard_map/ppermute | solution.py:436
  76.7 1.4 %collective-permute-start.26 = (f32[16,128]{1,0:T(8,128)S(1)}, f32[16,128]{1,0:T(8,128)S(1)}, u32[]{:S(2)}, u32[]{:S(2)}) collective-permute-start(f32[16,128]{1,0:T(8,128)S(1)} %slice.116), channel_id=1, source_target_pairs={{0,2},{1,3},{2,0},{3,1},{4,6},{5,7},{6,4},{7,5},{8,10},{9,11},{10,... | collective-permute-start | bytes 24584 | tf_op jit(solution)/shard_map/ppermute | solution.py:508
  78.3 1.6 %collective-permute-start.24 = (bf16[64,1024]{1,0:T(8,128)(2,1)S(1)}, bf16[64,1024]{1,0:T(8,128)(2,1)S(1)}, u32[]{:S(2)}, u32[]{:S(2)}) collective-permute-start(bf16[64,1024]{1,0:T(8,128)(2,1)S(1)} %get-tuple-element.84), channel_id=1, source_target_pairs={{0,2},{1,3},{2,0},{3,1},{4,6},{5,7},{6,4},{7,5},{8,10},{9,11},{10,... | collective-permute-start | bytes 393224 | tf_op jit(solution)/shard_map/ppermute | solution.py:450
  79.8 2.2 %collective-permute-done.26 = f32[16,128]{1,0:T(8,128)S(1)} collective-permute-done((f32[16,128]{1,0:T(8,128)S(1)}, f32[16,128]{1,0:T(8,128)S(1)}, u32[]{:S(2)}, u32[]{:S(2)}) %collective-permute-start.26) | collective-permute-done | bytes 8224 | tf_op jit(solution)/shard_map/ppermute | solution.py:508
  82.5 1.4 %collective-permute-start.27 = (f32[8,128]{1,0:T(8,128)S(1)}, f32[8,128]{1,0:T(8,128)S(1)}, u32[]{:S(2)}, u32[]{:S(2)}) collective-permute-start(f32[8,128]{1,0:T(8,128)S(1)} %shard_map.144), channel_id=1, source_target_pairs={{0,8},{4,12},{8,0},{12,4},{1,9},{5,13},{9,1},{13,5},{2,10},{6,14},... | collective-permute-start | bytes 12296 | tf_op jit(solution)/shard_map/ppermute | solution.py:532
  84.2 1.8 %shard_map.143 = bf16[128,2048]{1,0:T(8,128)(2,1)} custom-call(f32[64,1024]{1,0:T(8,128)S(1)} %get-tuple-element.94.refs_0_, f32[64,1024]{1,0:T(8,128)S(1)} %get-tuple-element.93.refs_1_, f32[64,1024]{1,0:T(8,128)S(1)} %get-tuple-element.92.refs_2_, bf16[128,1024]{1,0:T(8,128)(2,1)S(1)} %collective-permute-done.21.refs_3_, ...), custom_call_target="tpu_custom_call" | custom-call | flops 251658 | bytes 31457 | tf_op jit(solution)/shard_map/pallas_call | solution.py:370
  86.1 1.2 %collective-permute-done.28 = f32[8,128]{1,0:T(8,128)S(1)} collective-permute-done((f32[8,128]{1,0:T(8,128)S(1)}, f32[8,128]{1,0:T(8,128)S(1)}, u32[]{:S(2)}, u32[]{:S(2)}) %collective-permute-start.28) | collective-permute-done | bytes 4128 | tf_op jit(solution)/shard_map/ppermute | solution.py:532
  (64 shorter events, 16.2 us)
Async XLA Ops:
  1.7 9.3 %collective-permute-start.1 = (bf16[2,64,1024]{2,1,0:T(8,128)(2,1)S(1)}, bf16[2,64,1024]{2,1,0:T(8,128)(2,1)S(1)}, u32[]{:S(2)}, u32[]{:S(2)}) collective-permute-start(bf16[2,64,1024]{2,1,0:T(8,128)(2,1)S(1)} %get-tuple-element.96.refs_0_), channel_id=1, source_target_pairs={{0,8},{4,12},{8,0},{12,4},{1,9},{5,13},{9,1},{13,5},{2,10},{6,14},... | collective-permute-start | bytes 786440 | tf_op jit(solution)/shard_map/ppermute | solution.py:417
  4.7 8.1 %collective-permute-start = (bf16[2,64,1024]{2,1,0:T(8,128)(2,1)S(1)}, bf16[2,64,1024]{2,1,0:T(8,128)(2,1)S(1)}, u32[]{:S(2)}, u32[]{:S(2)}) collective-permute-start(bf16[2,64,1024]{2,1,0:T(8,128)(2,1)S(1)} %get-tuple-element.96.refs_0_), channel_id=1, source_target_pairs={{0,4},{4,0},{8,12},{12,8},{1,5},{5,1},{9,13},{13,9},{2,6},{6,2},{1... | collective-permute-start | bytes 786440 | tf_op jit(solution)/shard_map/ppermute | solution.py:417
  11.0 1.8 %collective-permute-start.2 = (bf16[2,64,1024]{2,1,0:T(8,128)(2,1)S(1)}, bf16[2,64,1024]{2,1,0:T(8,128)(2,1)S(1)}, u32[]{:S(2)}, u32[]{:S(2)}) collective-permute-start(bf16[2,64,1024]{2,1,0:T(8,128)(2,1)S(1)} %collective-permute-done.1.refs_2_), channel_id=1, source_target_pairs={{0,4},{4,0},{8,12},{12,8},{1,5},{5,1},{9,13},{13,9},{2,6},{6,2},{1... | collective-permute-start | bytes 786440 | tf_op jit(solution)/shard_map/ppermute | solution.py:417
  11.4 9.2 %collective-permute-start.4 = (bf16[2,64,1024]{2,1,0:T(8,128)(2,1)S(1)}, bf16[2,64,1024]{2,1,0:T(8,128)(2,1)S(1)}, u32[]{:S(2)}, u32[]{:S(2)}) collective-permute-start(bf16[2,64,1024]{2,1,0:T(8,128)(2,1)S(1)} %get-tuple-element.95.refs_0_.refs_4_), channel_id=1, source_target_pairs={{0,8},{4,12},{8,0},{12,4},{1,9},{5,13},{9,1},{13,5},{2,10},{6,14},... | collective-permute-start | bytes 786440 | tf_op jit(solution)/shard_map/ppermute | solution.py:417
  13.6 16.1 %collective-permute-start.9 = (bf16[256,1024]{1,0:T(8,128)(2,1)S(1)}, bf16[256,1024]{1,0:T(8,128)(2,1)S(1)}, u32[]{:S(2)}, u32[]{:S(2)}) collective-permute-start(bf16[256,1024]{1,0:T(8,128)(2,1)S(1)} %shard_map.131), channel_id=1, source_target_pairs={{0,16},{16,0},{1,17},{17,1},{2,18},{18,2},{3,19},{19,3},{4,20},{20... | collective-permute-start | bytes 1572872 | tf_op jit(solution)/shard_map/ppermute | solution.py:428
  15.2 5.3 %collective-permute-start.5 = (f32[128,256]{1,0:T(8,128)S(1)}, f32[128,256]{1,0:T(8,128)S(1)}, u32[]{:S(2)}, u32[]{:S(2)}) collective-permute-start(f32[128,256]{1,0:T(8,128)S(1)} %get-tuple-element.49), channel_id=1, source_target_pairs={{0,1},{1,0},{2,3},{3,2},{4,5},{5,4},{6,7},{7,6},{8,9},{9,8},{10,11... | collective-permute-start | bytes 393224 | tf_op jit(solution)/shard_map/ppermute | solution.py:472
  16.8 6.5 %collective-permute-start.3 = (bf16[2,64,1024]{2,1,0:T(8,128)(2,1)S(1)}, bf16[2,64,1024]{2,1,0:T(8,128)(2,1)S(1)}, u32[]{:S(2)}, u32[]{:S(2)}) collective-permute-start(bf16[2,64,1024]{2,1,0:T(8,128)(2,1)S(1)} %get-tuple-element.95.refs_0_.refs_4_), channel_id=1, source_target_pairs={{0,4},{4,0},{8,12},{12,8},{1,5},{5,1},{9,13},{13,9},{2,6},{6,2},{1... | collective-permute-start | bytes 786440 | tf_op jit(solution)/shard_map/ppermute | solution.py:417
  20.6 2.8 %collective-permute-start.6 = (bf16[2,64,1024]{2,1,0:T(8,128)(2,1)S(1)}, bf16[2,64,1024]{2,1,0:T(8,128)(2,1)S(1)}, u32[]{:S(2)}, u32[]{:S(2)}) collective-permute-start(bf16[2,64,1024]{2,1,0:T(8,128)(2,1)S(1)} %collective-permute-done.4.refs_2_.refs_6_), channel_id=1, source_target_pairs={{0,4},{4,0},{8,12},{12,8},{1,5},{5,1},{9,13},{13,9},{2,6},{6,2},{1... | collective-permute-start | bytes 786440 | tf_op jit(solution)/shard_map/ppermute | solution.py:417
  20.7 6.9 %collective-permute-start.7 = (f32[64,256]{1,0:T(8,128)S(1)}, f32[64,256]{1,0:T(8,128)S(1)}, u32[]{:S(2)}, u32[]{:S(2)}) collective-permute-start(f32[64,256]{1,0:T(8,128)S(1)} %slice.102), channel_id=1, source_target_pairs={{0,2},{1,3},{2,0},{3,1},{4,6},{5,7},{6,4},{7,5},{8,10},{9,11},{10,... | collective-permute-start | bytes 196616 | tf_op jit(solution)/shard_map/ppermute | solution.py:474
  24.2 19.8 %collective-permute-start.12 = (bf16[256,1024]{1,0:T(8,128)(2,1)S(1)}, bf16[256,1024]{1,0:T(8,128)(2,1)S(1)}, u32[]{:S(2)}, u32[]{:S(2)}) collective-permute-start(bf16[256,1024]{1,0:T(8,128)(2,1)S(1)} %shard_map.133), channel_id=1, source_target_pairs={{0,1},{1,0},{2,3},{3,2},{4,5},{5,4},{6,7},{7,6},{8,9},{9,8},{10,11... | collective-permute-start | bytes 1572872 | tf_op jit(solution)/shard_map/ppermute | solution.py:428
  28.0 4.0 %collective-permute-start.8 = (f32[1,64,128]{2,1,0:T(8,128)S(1)}, f32[1,64,128]{2,1,0:T(8,128)S(1)}, u32[]{:S(2)}, u32[]{:S(2)}) collective-permute-start(f32[1,64,128]{2,1,0:T(8,128)S(1)} %bitcast.11), channel_id=1, source_target_pairs={{0,16},{16,0},{1,17},{17,1},{2,18},{18,2},{3,19},{19,3},{4,20},{20... | collective-permute-start | bytes 98312 | tf_op jit(solution)/shard_map/ppermute | solution.py:486
  32.0 8.0 %collective-permute-start.10 = (f32[2,64,128]{2,1,0:T(8,128)S(1)}, f32[2,64,128]{2,1,0:T(8,128)S(1)}, u32[]{:S(2)}, u32[]{:S(2)}) collective-permute-start(f32[2,64,128]{2,1,0:T(8,128)S(1)} %pad_maximum_fusion.3), channel_id=1, source_target_pairs={{0,1},{1,0},{2,3},{3,2},{4,5},{5,4},{6,7},{7,6},{8,9},{9,8},{10,11... | collective-permute-start | bytes 196616 | tf_op jit(solution)/shard_map/ppermute | solution.py:488
  32.6 15.7 %collective-permute-start.14 = (bf16[256,1024]{1,0:T(8,128)(2,1)S(1)}, bf16[256,1024]{1,0:T(8,128)(2,1)S(1)}, u32[]{:S(2)}, u32[]{:S(2)}) collective-permute-start(bf16[256,1024]{1,0:T(8,128)(2,1)S(1)} %shard_map.132), channel_id=1, source_target_pairs={{0,16},{16,0},{1,17},{17,1},{2,18},{18,2},{3,19},{19,3},{4,20},{20... | collective-permute-start | bytes 1572872 | tf_op jit(solution)/shard_map/ppermute | solution.py:428
  40.0 5.8 %collective-permute-start.11 = (f32[2,64,128]{2,1,0:T(8,128)S(1)}, f32[2,64,128]{2,1,0:T(8,128)S(1)}, u32[]{:S(2)}, u32[]{:S(2)}) collective-permute-start(f32[2,64,128]{2,1,0:T(8,128)S(1)} %fusion), channel_id=1, source_target_pairs={{0,2},{1,3},{2,0},{3,1},{4,6},{5,7},{6,4},{7,5},{8,10},{9,11},{10,... | collective-permute-start | bytes 196616 | tf_op jit(solution)/shard_map/ppermute | solution.py:488
  41.6 11.5 %collective-permute-start.17 = (bf16[128,1024]{1,0:T(8,128)(2,1)S(1)}, bf16[128,1024]{1,0:T(8,128)(2,1)S(1)}, u32[]{:S(2)}, u32[]{:S(2)}) collective-permute-start(bf16[128,1024]{1,0:T(8,128)(2,1)S(1)} %get-tuple-element.71), channel_id=1, source_target_pairs={{0,1},{1,0},{2,3},{3,2},{4,5},{5,4},{6,7},{7,6},{8,9},{9,8},{10,11... | collective-permute-start | bytes 786440 | tf_op jit(solution)/shard_map/ppermute | solution.py:436
  45.8 7.1 %collective-permute-start.13 = (f32[2,64,128]{2,1,0:T(8,128)S(1)}, f32[2,64,128]{2,1,0:T(8,128)S(1)}, u32[]{:S(2)}, u32[]{:S(2)}) collective-permute-start(f32[2,64,128]{2,1,0:T(8,128)S(1)} %fusion.1), channel_id=1, source_target_pairs={{0,8},{4,12},{8,0},{12,4},{1,9},{5,13},{9,1},{13,5},{2,10},{6,14},... | collective-permute-start | bytes 196616 | tf_op jit(solution)/shard_map/ppermute | solution.py:496
  47.3 14.8 %collective-permute-start.19 = (bf16[256,1024]{1,0:T(8,128)(2,1)S(1)}, bf16[256,1024]{1,0:T(8,128)(2,1)S(1)}, u32[]{:S(2)}, u32[]{:S(2)}) collective-permute-start(bf16[256,1024]{1,0:T(8,128)(2,1)S(1)} %shard_map.135), channel_id=1, source_target_pairs={{0,16},{16,0},{1,17},{17,1},{2,18},{18,2},{3,19},{19,3},{4,20},{20... | collective-permute-start | bytes 1572872 | tf_op jit(solution)/shard_map/ppermute | solution.py:428
  49.2 12.6 %collective-permute-start.18 = (bf16[128,1024]{1,0:T(8,128)(2,1)S(1)}, bf16[128,1024]{1,0:T(8,128)(2,1)S(1)}, u32[]{:S(2)}, u32[]{:S(2)}) collective-permute-start(bf16[128,1024]{1,0:T(8,128)(2,1)S(1)} %get-tuple-element.72), channel_id=1, source_target_pairs={{0,1},{1,0},{2,3},{3,2},{4,5},{5,4},{6,7},{7,6},{8,9},{9,8},{10,11... | collective-permute-start | bytes 786440 | tf_op jit(solution)/shard_map/ppermute | solution.py:436
  50.5 17.2 %collective-permute-start.21 = (bf16[128,1024]{1,0:T(8,128)(2,1)S(1)}, bf16[128,1024]{1,0:T(8,128)(2,1)S(1)}, u32[]{:S(2)}, u32[]{:S(2)}) collective-permute-start(bf16[128,1024]{1,0:T(8,128)(2,1)S(1)} %get-tuple-element.81), channel_id=1, source_target_pairs={{0,2},{1,3},{2,0},{3,1},{4,6},{5,7},{6,4},{7,5},{8,10},{9,11},{10,... | collective-permute-start | bytes 786440 | tf_op jit(solution)/shard_map/ppermute | solution.py:436
  52.9 1.4 %collective-permute-start.15 = (f32[4,64,128]{2,1,0:T(8,128)S(1)}, f32[4,64,128]{2,1,0:T(8,128)S(1)}, u32[]{:S(2)}, u32[]{:S(2)}) collective-permute-start(f32[4,64,128]{2,1,0:T(8,128)S(1)} %pad_maximum_fusion.2), channel_id=1, source_target_pairs={{0,4},{4,0},{8,12},{12,8},{1,5},{5,1},{9,13},{13,9},{2,6},{6,2},{1... | collective-permute-start | bytes 393224 | tf_op jit(solution)/shard_map/ppermute | solution.py:496
  57.4 10.3 %collective-permute-start.16 = (f32[16,512]{1,0:T(8,128)S(1)}, f32[16,512]{1,0:T(8,128)S(1)}, u32[]{:S(2)}, u32[]{:S(2)}) collective-permute-start(f32[16,512]{1,0:T(8,128)S(1)} %slice.104), channel_id=1, source_target_pairs={{0,16},{16,0},{1,17},{17,1},{2,18},{18,2},{3,19},{19,3},{4,20},{20... | collective-permute-start | bytes 98312 | tf_op jit(solution)/shard_map/ppermute | solution.py:508
  61.8 13.3 %collective-permute-start.20 = (bf16[64,2048]{1,0:T(8,128)(2,1)S(1)}, bf16[64,2048]{1,0:T(8,128)(2,1)S(1)}, u32[]{:S(2)}, u32[]{:S(2)}) collective-permute-start(bf16[64,2048]{1,0:T(8,128)(2,1)S(1)} %pad_maximum_fusion.1), channel_id=1, source_target_pairs={{0,2},{1,3},{2,0},{3,1},{4,6},{5,7},{6,4},{7,5},{8,10},{9,11},{10,... | collective-permute-start | bytes 786440 | tf_op jit(solution)/shard_map/ppermute | solution.py:450
  63.1 13.4 %collective-permute-start.23 = (bf16[128,1024]{1,0:T(8,128)(2,1)S(1)}, bf16[128,1024]{1,0:T(8,128)(2,1)S(1)}, u32[]{:S(2)}, u32[]{:S(2)}) collective-permute-start(bf16[128,1024]{1,0:T(8,128)(2,1)S(1)} %get-tuple-element.83), channel_id=1, source_target_pairs={{0,1},{1,0},{2,3},{3,2},{4,5},{5,4},{6,7},{7,6},{8,9},{9,8},{10,11... | collective-permute-start | bytes 786440 | tf_op jit(solution)/shard_map/ppermute | solution.py:436
  72.0 4.8 %collective-permute-start.25 = (f32[16,256]{1,0:T(8,128)S(1)}, f32[16,256]{1,0:T(8,128)S(1)}, u32[]{:S(2)}, u32[]{:S(2)}) collective-permute-start(f32[16,256]{1,0:T(8,128)S(1)} %slice.114), channel_id=1, source_target_pairs={{0,1},{1,0},{2,3},{3,2},{4,5},{5,4},{6,7},{7,6},{8,9},{9,8},{10,11... | collective-permute-start | bytes 49160 | tf_op jit(solution)/shard_map/ppermute | solution.py:508
  72.6 11.3 %collective-permute-start.22 = (bf16[64,1024]{1,0:T(8,128)(2,1)S(1)}, bf16[64,1024]{1,0:T(8,128)(2,1)S(1)}, u32[]{:S(2)}, u32[]{:S(2)}) collective-permute-start(bf16[64,1024]{1,0:T(8,128)(2,1)S(1)} %get-tuple-element.82), channel_id=1, source_target_pairs={{0,16},{16,0},{1,17},{17,1},{2,18},{18,2},{3,19},{19,3},{4,20},{20... | collective-permute-start | bytes 393224 | tf_op jit(solution)/shard_map/ppermute | solution.py:450
  76.7 5.4 %collective-permute-start.26 = (f32[16,128]{1,0:T(8,128)S(1)}, f32[16,128]{1,0:T(8,128)S(1)}, u32[]{:S(2)}, u32[]{:S(2)}) collective-permute-start(f32[16,128]{1,0:T(8,128)S(1)} %slice.116), channel_id=1, source_target_pairs={{0,2},{1,3},{2,0},{3,1},{4,6},{5,7},{6,4},{7,5},{8,10},{9,11},{10,... | collective-permute-start | bytes 24584 | tf_op jit(solution)/shard_map/ppermute | solution.py:508
  78.3 5.9 %collective-permute-start.24 = (bf16[64,1024]{1,0:T(8,128)(2,1)S(1)}, bf16[64,1024]{1,0:T(8,128)(2,1)S(1)}, u32[]{:S(2)}, u32[]{:S(2)}) collective-permute-start(bf16[64,1024]{1,0:T(8,128)(2,1)S(1)} %get-tuple-element.84), channel_id=1, source_target_pairs={{0,2},{1,3},{2,0},{3,1},{4,6},{5,7},{6,4},{7,5},{8,10},{9,11},{10,... | collective-permute-start | bytes 393224 | tf_op jit(solution)/shard_map/ppermute | solution.py:450
  82.5 3.6 %collective-permute-start.27 = (f32[8,128]{1,0:T(8,128)S(1)}, f32[8,128]{1,0:T(8,128)S(1)}, u32[]{:S(2)}, u32[]{:S(2)}) collective-permute-start(f32[8,128]{1,0:T(8,128)S(1)} %shard_map.144), channel_id=1, source_target_pairs={{0,8},{4,12},{8,0},{12,4},{1,9},{5,13},{9,1},{13,5},{2,10},{6,14},... | collective-permute-start | bytes 12296 | tf_op jit(solution)/shard_map/ppermute | solution.py:532
  86.1 1.2 %collective-permute-start.28 = (f32[8,128]{1,0:T(8,128)S(1)}, f32[8,128]{1,0:T(8,128)S(1)}, u32[]{:S(2)}, u32[]{:S(2)}) collective-permute-start(f32[8,128]{1,0:T(8,128)S(1)} %add.70), channel_id=1, source_target_pairs={{0,4},{4,0},{8,12},{12,8},{1,5},{5,1},{9,13},{13,9},{2,6},{6,2},{1... | collective-permute-start | bytes 12296 | tf_op jit(solution)/shard_map/ppermute | solution.py:532
